TPU v7x, 256 devices: a whole 4x4x8 slice. The times are simulated.
256 devices in a mesh: dp: 4 (over x), vocab: 64 (over z, y, core).
Axes of the slice: x: 4, y: 4, z: 8, core: 2. Of those that a mesh axis runs over, the one named last changes fastest.
Arguments:
- hidden_t: bfloat16 [8192, 768], P(('dp', 'vocab')), may hold values from -6 to 6
- head: bfloat16 [8192, 81920], P('dp', 'vocab'), may hold values from -0.2 to 0.2
- teacher: bfloat16 [768, 81920], P('dp', 'vocab'), may hold values from -16 to 960
- labels: int32 [768], P('dp'), may hold values from 0 to 81919
- temps: float32 [4], replicated, may hold values from 1 to 4
- mix: float32 [2], replicated, may hold values from 0.3 to 1
Outputs:
- hidden_grad: float32 [8192, 768], P(('dp', 'vocab'))
- head_grad: bfloat16 [8192, 81920], P('dp', 'vocab')
All inputs are finite; a program needn't handle non-finite values.
Results may differ from a plain program's by a relative error of at most 0.012.
Values may be sent and summed in bfloat16 or wider, within the bound.
A program may use at most 128 MiB of HBM per device.

v0:
```python
import jax
import jax.numpy as jnp
from jax import lax
from jax.sharding import PartitionSpec as P


def shards(hidden_t, head, teacher, labels, temps, mix):
    h_block = lax.all_gather(hidden_t, "vocab", axis=0, tiled=True)
    block_width = head.shape[1]
    logits = lax.psum_scatter(
        lax.dot_general(
            h_block, head, (((0,), (0,)), ((), ())), preferred_element_type=jnp.float32
        ),
        "dp",
        scatter_dimension=0,
        tiled=True,
    )
    target = teacher.astype(jnp.float32)
    inverse = 1.0 / temps
    student = jnp.concatenate([logits[None], logits[None] * inverse[:, None, None]], axis=0)
    teacher_scaled = target[None] * inverse[:, None, None]
    stacked = jnp.concatenate([student, teacher_scaled], axis=0)
    local_peak = jnp.max(stacked, axis=2)
    highest = lax.pmax(local_peak, "vocab")
    summed = lax.psum(jnp.sum(jnp.exp(stacked - highest[:, :, None]), axis=2), "vocab")
    softmaxes = jnp.exp(stacked - highest[:, :, None]) / summed[:, :, None]
    offset = lax.axis_index("vocab") * block_width
    columns = jnp.arange(block_width, dtype=jnp.int32)[None, :] + offset
    onehot = (columns == labels[:, None]).astype(jnp.float32)
    heat_count = temps.shape[0]
    logit_grad = mix[0] * (softmaxes[0] - onehot)
    weights = mix[1] * temps
    logit_grad = logit_grad + jnp.einsum(
        "k,kab->ab", weights, softmaxes[1 : 1 + heat_count] - softmaxes[1 + heat_count :]
    )
    logit_grad = logit_grad.astype(jnp.bfloat16)
    grad_all = lax.all_gather(logit_grad, "dp", axis=0, tiled=True)
    head_grad = jnp.dot(h_block, grad_all, preferred_element_type=jnp.float32).astype(jnp.bfloat16)
    hidden_grad = lax.psum_scatter(
        lax.dot_general(
            head, grad_all, (((1,), (1,)), ((), ())), preferred_element_type=jnp.float32
        ),
        "vocab",
        scatter_dimension=0,
        tiled=True,
    )
    return (hidden_grad, head_grad)


def solution(mesh):
    placed = (P(("dp", "vocab"), None), P("dp", "vocab"), P("dp", "vocab"), P("dp"), P(), P())
    return jax.shard_map(
        shards,
        mesh=mesh,
        in_specs=placed,
        out_specs=(P(("dp", "vocab"), None), P("dp", "vocab")),
        check_vma=False,
    )
```

profile of v0, /device:TPU:2, one launch (start us, length us, event | category | flops | bytes accessed | tf_op | source)
XLA Modules:
  0.0 861.4 jit_solution(14187076467342216205)
XLA Ops:
  7.2 0.0 all-gather.3.cloned.1.call-start
  7.2 0.7 all-gather.3.cloned.1.call-update
  7.9 0.0 copy-start.3
  7.9 0.0 reduce-scatter.5.cloned.1.call-start
  8.0 83.8 %all-gather.3.cloned.1.call-done = bf16[2048,768]{1,0:T(8,128)(2,1)} async-done(((bf16[32,768]{1,0:T(8,128)(2,1)}), bf16[2048,768]{1,0:T(8,128)(2,1)}) %all-gather.3.cloned.1.call-update) | async-done | bytes 3145744 | tf_op jit(solution)/shard_map/all_gather | solution.py:8
  91.7 9.7 %fusion.14 = f32[768,1280]{1,0:T(8,128)} fusion(bf16[2048,768]{1,0:T(8,128)(2,1)} %all-gather.3.cloned.1.call-done, bf16[2048,1280]{1,0:T(8,128)(2,1)} %param.7), kind=kOutput, calls=%fused_computation.24 | convolution fusion | flops 4026531840 | bytes 12320768 | tf_op jit(solution)/shard_map/dot_general | solution.py:11
  101.4 0.0 copy-start.4
  101.4 0.0 copy-start.7
  101.4 0.0 reduce-scatter.5.cloned.1.call-update
  101.4 0.0 all-gather.5.cloned.1.call-start
  101.5 0.0 copy-done.3
  101.5 0.1 convert_element_type.15
  101.6 0.5 copy-done.4
  102.0 0.6 fusion.13
  102.7 0.0 copy-done.7
  102.7 42.3 %reduce-scatter.5.cloned.1.call-done = f32[192,1280]{1,0:T(8,128)} async-done(((f32[768,1280]{1,0:T(8,128)}), f32[192,1280]{1,0:T(8,128)}) %reduce-scatter.5.cloned.1.call-update) | async-done | bytes 983056 | tf_op jit(solution)/shard_map/reduce_scatter | solution.py:10
  145.0 0.0 copy-start.2
  145.0 2.0 broadcast_multiply_fusion.1
  147.0 0.0 copy-start
  147.0 0.0 copy-start.1
  147.0 1.8 copy-done
  148.9 1.4 copy-done.1
  150.2 0.0 copy-done.2
  150.2 0.8 fusion.5
  151.0 251.0 %pmax.7 = f32[9,192]{1,0:T(8,128)S(1)} all-reduce(f32[9,192]{1,0:T(8,128)S(1)} %fusion.5), channel_id=1, replica_groups=mesh['dp'=4,'vocab'=64] {'vocab'}, use_global_device_ids=true, to_apply=%region_2.0 | all-reduce | flops 1728 | bytes 13824 | tf_op jit(solution)/shard_map/pmax | solution.py:24
  402.0 4.3 fusion.1
  406.3 246.1 %psum.7 = f32[9,192]{1,0:T(8,128)S(1)} all-reduce(f32[9,192]{1,0:T(8,128)S(1)} %fusion.1), channel_id=1, replica_groups=mesh['dp'=4,'vocab'=64] {'vocab'}, use_global_device_ids=true, to_apply=%region_4.0 | all-reduce | flops 1728 | bytes 13824 | tf_op jit(solution)/shard_map/psum | solution.py:25
  652.5 4.6 fusion
  657.1 0.0 copy-start.5
  657.1 0.5 slice_subtract_fusion
  657.6 2.2 fusion.3
  659.8 0.0 copy-done.5
  659.8 1.7 fusion.9
  661.5 0.0 all-gather.5.cloned.1.call-update
  661.5 0.2 reduce-scatter.7.cloned.1.call-start
  661.7 27.0 %all-gather.5.cloned.1.call-done = bf16[768,1280]{1,0:T(8,128)(2,1)} async-done(((bf16[192,1280]{1,0:T(8,128)(2,1)}), bf16[768,1280]{1,0:T(8,128)(2,1)}) %all-gather.5.cloned.1.call-update) | async-done | bytes 1966096 | tf_op jit(solution)/shard_map/all_gather | solution.py:37
  688.7 10.0 %convolution_bitcast_fusion = f32[2048,768]{0,1:T(8,128)} fusion(bf16[768,1280]{1,0:T(8,128)(2,1)} %all-gather.5.cloned.1.call-done, bf16[2048,1280]{1,0:T(8,128)(2,1)} %param.7), kind=kOutput, calls=%fused_computation.9 | convolution fusion | flops 4026531840 | bytes 13500416 | tf_op jit(solution)/shard_map/dot_general | solution.py:40
  698.7 6.6 copy.16
  705.3 0.0 copy-start.6
  705.3 0.0 reduce-scatter.7.cloned.1.call-update
  705.3 1.9 copy-done.6
  707.2 7.6 fusion.2
  714.8 8.0 copy.13
  722.7 132.1 %reduce-scatter.7.cloned.1.call-done = f32[32,768]{1,0:T(8,128)} async-done(((f32[2048,768]{1,0:T(8,128)}), f32[32,768]{1,0:T(8,128)}) %reduce-scatter.7.cloned.1.call-update) | async-done | bytes 98320
  (2 shorter events, 0.0 us)
Async XLA Ops:
  7.2 84.6 %all-gather.3.cloned.1.call-start = ((), (), s32[]{:S(2)}) async-start(), calls=%async_computation.2 | async-start | bytes 3194880 | tf_op jit(solution)/shard_map/all_gather | solution.py:8
  7.9 93.6 %copy-start.3 = (bf16[192,1280]{1,0:T(8,128)(2,1)S(1)}, bf16[192,1280]{1,0:T(8,128)(2,1)}, u32[]{:S(2)}) copy-start(bf16[192,1280]{1,0:T(8,128)(2,1)} %param.8) | copy-start | bytes 1474564
  7.9 137.1 %reduce-scatter.5.cloned.1.call-start = ((), (), s32[]{:S(2)}) async-start(), calls=%async_computation.3 | async-start | bytes 4915200 | tf_op jit(solution)/shard_map/reduce_scatter | solution.py:10
  101.4 0.7 copy-start.4
  101.4 1.3 copy-start.7
  101.4 587.3 %all-gather.5.cloned.1.call-start = ((), (), s32[]{:S(2)}) async-start(), calls=%async_computation.4 | async-start | bytes 2457600 | tf_op jit(solution)/shard_map/all_gather | solution.py:37
  145.0 5.3 copy-start.2
  147.0 1.9 copy-start
  147.0 3.2 copy-start.1
  657.1 2.7 copy-start.5
  661.5 193.4 %reduce-scatter.7.cloned.1.call-start = ((), (), s32[]{:S(2)}) async-start(), calls=%async_computation.5 | async-start | bytes 6389760
  705.3 1.9 copy-start.6
Sparse Core Ops, SparseCore 0:
  10.7 80.9 all-gather.2
  101.5 43.3 reduce-scatter.4
  661.6 27.0 all-gather.4
  705.5 149.3 reduce-scatter.6
where the time goes:
time: 862 us; the launch traced here: 861 us
  blocking collectives  497 us (58%)
  waiting for transfers between devices  286 us (33%)
  matrix products  29.5 us (3%)
  local copies, waits for them, and re-layouts  20.7 us (2%)
  other arithmetic  13.9 us (2%)
  between operations  13.9 us (2%)
    pmax x1, blocking collectives, shards(): highest = lax.pmax(local_peak, 'vocab')  251 us
    psum x1, blocking collectives, shards(): lax.psum(jnp.sum(jnp.exp(stacked - highest[:, :, None]), axis=2), 'vocab')  246 us
    unnamed x5, waiting for transfers between devices  133 us
    all_gather x1, waiting for transfers between devices, shards(): h_block = lax.all_gather(hidden_t, 'vocab', axis=0, tiled=True)  83.8 us
    reduce_scatter x1, waiting for transfers between devices, shards(): lax.psum_scatter(lax.dot_general(h_block, head, (((0,), (0,)), ((), ())),...  42.3 us
    all_gather x1, waiting for transfers between devices, shards(): grad_all = lax.all_gather(logit_grad, 'dp', axis=0, tiled=True)  27 us
    unnamed x18, local copies, waits for them, and re-layouts  20.1 us
  transfers between devices with their start and end apart: 4, of which 4 were waited for; matrix products, arithmetic and copies ran while one was open for 2% of the time, Pallas kernels for 0%

commit v1 on v0

v1 whole, which is shorter than its diff:
```python
import jax
import jax.numpy as jnp
from jax import lax
from jax.sharding import PartitionSpec as P


def shards(hidden_t, head, teacher, labels, temps, mix):
    h_block = lax.all_gather(hidden_t, "vocab", axis=0, tiled=True)
    block_width = head.shape[1]
    logits = lax.psum_scatter(
        lax.dot_general(
            h_block, head, (((0,), (0,)), ((), ())), preferred_element_type=jnp.float32
        ),
        "dp",
        scatter_dimension=0,
        tiled=True,
    )
    target = teacher.astype(jnp.float32)
    inverse = 1.0 / temps
    heat_count = temps.shape[0]
    all_inverse = jnp.concatenate([jnp.ones((1,), jnp.float32), inverse])
    student_peak = jnp.max(logits, axis=1)
    teacher_peak = jnp.max(target, axis=1)
    parts = [student_peak, teacher_peak]
    for k in range(1 + heat_count):
        parts.append(jnp.sum(jnp.exp((logits - student_peak[:, None]) * all_inverse[k]), axis=1))
    for k in range(heat_count):
        parts.append(jnp.sum(jnp.exp((target - teacher_peak[:, None]) * inverse[k]), axis=1))
    gathered = lax.all_gather(jnp.stack(parts), "vocab", axis=0)
    top = jnp.max(gathered[:, :2], axis=0)
    gap = gathered[:, :2] - top[None]
    denominators = []
    for k in range(1 + heat_count):
        denominators.append(jnp.sum(gathered[:, 2 + k] * jnp.exp(gap[:, 0] * all_inverse[k]), axis=0))
    for k in range(heat_count):
        denominators.append(
            jnp.sum(gathered[:, 3 + heat_count + k] * jnp.exp(gap[:, 1] * inverse[k]), axis=0)
        )
    columns = jnp.arange(block_width, dtype=jnp.int32)[None, :] + lax.axis_index("vocab") * block_width
    s_off = logits - top[0][:, None]
    t_off = target - top[1][:, None]
    grad = jnp.exp(s_off) * (mix[0] / denominators[0])[:, None]
    grad = grad - jnp.where(columns == labels[:, None], mix[0], 0.0)
    for k in range(heat_count):
        w = mix[1] * temps[k]
        grad = grad + jnp.exp(s_off * inverse[k]) * (w / denominators[1 + k])[:, None]
        grad = grad - jnp.exp(t_off * inverse[k]) * (w / denominators[1 + heat_count + k])[:, None]
    grad = grad.astype(jnp.bfloat16)
    grad_all = lax.all_gather(grad, "dp", axis=0, tiled=True)
    hidden_grad = lax.psum_scatter(
        lax.dot_general(
            head, grad_all, (((1,), (1,)), ((), ())), preferred_element_type=jnp.float32
        ),
        "vocab",
        scatter_dimension=0,
        tiled=True,
    )
    head_grad = jnp.dot(h_block, grad_all, preferred_element_type=jnp.float32).astype(jnp.bfloat16)
    return (hidden_grad, head_grad)


def solution(mesh):
    placed = (P(("dp", "vocab"), None), P("dp", "vocab"), P("dp", "vocab"), P("dp"), P(), P())
    return jax.shard_map(
        shards,
        mesh=mesh,
        in_specs=placed,
        out_specs=(P(("dp", "vocab"), None), P("dp", "vocab")),
        check_vma=False,
    )
```

time: 862 us -> 417 us (0.48)
  blocking collectives: 497 us -> 51.4 us
    pmax x1 -> x0, blocking collectives: 251 us -> none  [shards(): highest = lax.pmax(local_peak, 'vocab')]
    psum x1 -> x0, blocking collectives: 246 us -> none  [shards(): lax.psum(jnp.sum(jnp.exp(stacked - highest[:, :, None]), axis=2), 'vocab')]
    all_gather x0 -> x1, blocking collectives: none -> 51.4 us  [shards(): gathered = lax.all_gather(jnp.stack(parts), 'vocab', axis=0)]
    unnamed x18 -> x14, local copies, waits for them, and re-layouts: 20.1 us -> 17.4 us
  transfers between devices with their start and end apart: 4 -> 4, of which waited for: 4 -> 4; matrix products, arithmetic and copies ran while one was open for 2% -> 4% of each run, Pallas kernels for 0% -> 0%
where the time goes in v1:
time: 417 us; the launch traced here: 416 us
  waiting for transfers between devices  282 us (68%)
  blocking collectives  51.4 us (12%)
  matrix products  27.3 us (7%)
  between operations  19 us (5%)
  local copies, waits for them, and re-layouts  18.8 us (5%)
  other arithmetic  17.6 us (4%)
    unnamed x5, waiting for transfers between devices  133 us
    all_gather x1, waiting for transfers between devices, shards(): h_block = lax.all_gather(hidden_t, 'vocab', axis=0, tiled=True)  83.8 us
    all_gather x1, blocking collectives, shards(): gathered = lax.all_gather(jnp.stack(parts), 'vocab', axis=0)  51.4 us
    reduce_scatter x1, waiting for transfers between devices, shards(): lax.psum_scatter(lax.dot_general(h_block, head, (((0,), (0,)), ((), ())),...  35.9 us
    all_gather x1, waiting for transfers between devices, shards(): grad_all = lax.all_gather(grad, 'dp', axis=0, tiled=True)  29.2 us
    unnamed x14, local copies, waits for them, and re-layouts  17.4 us
    dot_general x1, matrix products, shards(): lax.dot_general(head, grad_all, (((1,), (1,)), ((), ())), preferred_eleme...  9.99 us
    dot_general x1, matrix products, shards(): lax.dot_general(h_block, head, (((0,), (0,)), ((), ())), preferred_elemen...  9.69 us
  transfers between devices with their start and end apart: 4, of which 4 were waited for; matrix products, arithmetic and copies ran while one was open for 4% of the time, Pallas kernels for 0%

profile of v1, /device:TPU:2, one launch (start us, length us, event | category | flops | bytes accessed | tf_op | source)
XLA Modules:
  0.0 416.1 jit_solution(3670360584585135404)
XLA Ops:
  7.2 0.0 all-gather.5.cloned.1.call-start
  7.2 0.7 all-gather.5.cloned.1.call-update
  7.9 0.0 reduce-scatter.5.cloned.1.call-start
  7.9 83.8 %all-gather.5.cloned.1.call-done = bf16[2048,768]{1,0:T(8,128)(2,1)} async-done(((bf16[32,768]{1,0:T(8,128)(2,1)}), bf16[2048,768]{1,0:T(8,128)(2,1)}) %all-gather.5.cloned.1.call-update) | async-done | bytes 3145744 | tf_op jit(solution)/shard_map/all_gather | solution.py:8
  91.7 9.7 %fusion.46 = f32[768,1280]{1,0:T(8,128)} fusion(bf16[2048,768]{1,0:T(8,128)(2,1)} %all-gather.5.cloned.1.call-done, bf16[2048,1280]{1,0:T(8,128)(2,1)} %param.7), kind=kOutput, calls=%fused_computation.77 | convolution fusion | flops 4026531840 | bytes 12320768 | tf_op jit(solution)/shard_map/dot_general | solution.py:11
  101.4 0.0 copy-start.1
  101.4 0.0 copy-start.2
  101.4 0.0 copy-start.3
  101.4 0.0 reduce-scatter.5.cloned.1.call-update
  101.4 0.0 all-gather.7.cloned.1.call-start
  101.5 0.9 copy-done.1
  102.4 0.0 copy-start.5
  102.4 0.1 reduce_max.37
  102.6 0.0 copy-done.2
  102.6 0.0 copy-done.3
  102.6 0.7 fusion.43
  108.4 0.7 fusion.45
  109.1 35.9 %reduce-scatter.5.cloned.1.call-done = f32[192,1280]{1,0:T(8,128)} async-done(((f32[768,1280]{1,0:T(8,128)}), f32[192,1280]{1,0:T(8,128)}) %reduce-scatter.5.cloned.1.call-update) | async-done | bytes 983056 | tf_op jit(solution)/shard_map/reduce_scatter | solution.py:10
  145.0 0.0 copy-start
  145.0 1.4 reduce_max.36
  146.4 5.2 %fusion.32 = (f32[192]{0:T(256)S(1)}, f32[192]{0:T(256)S(1)}, f32[192]{0:T(256)S(1)}, f32[192]{0:T(256)S(1)}, f32[192]{0:T(256)S(1)}, /*index=5*/f32[192]{0:T(25...) fusion(bf16[192,1280]{1,0:T(8,128)(2,1)S(1)} %copy-done.1, f32[192]{0:T(256)S(1)} %reduce_max.42, f32[]{:T(128)} %bitcast.9, ...), kind=kLoop, calls=%fused_computation.36 | loop fusion | flops 4913472 | bytes 1483024 | tf_op jit(solution)/shard_map/reduce_sum | solution.py:28
  151.7 0.1 stack.44
  151.7 51.4 %all-gather.1 = f32[64,11,192]{2,1,0:T(8,128)S(1)} all-gather(f32[1,11,192]{2,1,0:T(8,128)S(1)} %bitcast.34), channel_id=2, replica_groups=mesh['dp'=4,'vocab'=64] {'vocab'}, dimensions={0}, use_global_device_ids=true | all-gather | bytes 549120 | tf_op jit(solution)/shard_map/all_gather | solution.py:29
  203.1 0.1 slice_reduce_fusion
  203.2 0.1 slice_subtract_fusion
  203.3 3.9 fusion.33
  207.3 0.7 broadcast_divide_fusion.8
  207.9 0.0 copy-done.5
  207.9 0.0 copy-done
  208.0 6.0 %fusion.18 = bf16[192,1280]{1,0:T(8,128)(2,1)} fusion(bf16[192,1280]{1,0:T(8,128)(2,1)S(1)} %copy-done.1, f32[192,1280]{1,0:T(8,128)S(1)} %copy-done, f32[192]{0:T(256)S(1)} %broadcast_divide_fusion, f32[192]{0:T(256)S(1)} %broadcast_divide_fusion.1, f32[192]{0:T(256)S(1)} %broadcast_divide_fusion.2, f32[192]{0:T(256)S(1)} %broadcast_divide_fusion.3, ...), kind=kLoop, calls=%fused_computation.22 | loop fusion | flops 7864320 | bytes 1980436 | tf_op jit(solution)/shard_map/convert_element_type | solution.py:48
  213.9 0.0 all-gather.7.cloned.1.call-update
  213.9 0.2 reduce-scatter.7.cloned.1.call-start
  214.2 29.2 %all-gather.7.cloned.1.call-done = bf16[768,1280]{1,0:T(8,128)(2,1)} async-done(((bf16[192,1280]{1,0:T(8,128)(2,1)}), bf16[768,1280]{1,0:T(8,128)(2,1)}) %all-gather.7.cloned.1.call-update) | async-done | bytes 1966096 | tf_op jit(solution)/shard_map/all_gather | solution.py:49
  243.4 10.0 %convolution_bitcast_fusion = f32[2048,768]{0,1:T(8,128)} fusion(bf16[768,1280]{1,0:T(8,128)(2,1)} %all-gather.7.cloned.1.call-done, bf16[2048,1280]{1,0:T(8,128)(2,1)} %param.7), kind=kOutput, calls=%fused_computation.2 | convolution fusion | flops 4026531840 | bytes 13500416 | tf_op jit(solution)/shard_map/dot_general | solution.py:51
  253.3 6.6 %copy.12 = f32[2048,768]{1,0:T(8,128)} copy(f32[2048,768]{0,1:T(8,128)} %convolution_bitcast_fusion) | data formatting | bytes 12582912
  259.9 0.0 copy-start.4
  259.9 0.0 reduce-scatter.7.cloned.1.call-update
  260.0 1.9 copy-done.4
  261.8 7.7 %fusion = bf16[2048,1280]{0,1:T(8,128)(2,1)} fusion(bf16[768,1280]{1,0:T(8,128)(2,1)} %all-gather.7.cloned.1.call-done, bf16[2048,768]{1,0:T(8,128)(2,1)S(1)} %copy-done.4), kind=kOutput, calls=%fused_computation.1 | convolution fusion | flops 4029153280 | bytes 10354688 | tf_op jit(solution)/shard_map/dot_general | solution.py:58
  269.5 7.9 %copy.11 = bf16[2048,1280]{1,0:T(8,128)(2,1)} copy(bf16[2048,1280]{0,1:T(8,128)(2,1)} %fusion) | data formatting | bytes 10485760
  277.4 132.1 %reduce-scatter.7.cloned.1.call-done = f32[32,768]{1,0:T(8,128)} async-done(((f32[2048,768]{1,0:T(8,128)}), f32[32,768]{1,0:T(8,128)}) %reduce-scatter.7.cloned.1.call-update) | async-done | bytes 98320
  (12 shorter events, 0.1 us)
Async XLA Ops:
  7.2 84.6 %all-gather.5.cloned.1.call-start = ((), (), s32[]{:S(2)}) async-start(), calls=%async_computation.2 | async-start | bytes 3194880 | tf_op jit(solution)/shard_map/all_gather | solution.py:8
  7.9 137.1 %reduce-scatter.5.cloned.1.call-start = ((), (), s32[]{:S(2)}) async-start(), calls=%async_computation.3 | async-start | bytes 4915200 | tf_op jit(solution)/shard_map/reduce_scatter | solution.py:10
  101.4 1.0 copy-start.1
  101.4 1.2 copy-start.2
  101.4 1.2 copy-start.3
  101.4 141.9 %all-gather.7.cloned.1.call-start = ((), (), s32[]{:S(2)}) async-start(), calls=%async_computation.4 | async-start | bytes 2457600 | tf_op jit(solution)/shard_map/all_gather | solution.py:49
  102.4 105.5 %copy-start.5 = (s32[192]{0:T(256)S(1)}, s32[192]{0:T(256)}, u32[]{:S(2)}) copy-start(s32[192]{0:T(256)} %param.9) | copy-start | bytes 2308
  145.0 62.9 %copy-start = (f32[192,1280]{1,0:T(8,128)S(1)}, f32[192,1280]{1,0:T(8,128)}, u32[]{:S(2)}) copy-start(f32[192,1280]{1,0:T(8,128)} %reduce-scatter.5.cloned.1.call-done) | copy-start | bytes 2949124
  213.9 195.6 %reduce-scatter.7.cloned.1.call-start = ((), (), s32[]{:S(2)}) async-start(), calls=%async_computation.5 | async-start | bytes 6389760
  259.9 1.9 copy-start.4
Sparse Core Ops, SparseCore 0:
  10.7 80.9 all-gather.4
  101.6 43.3 reduce-scatter.4
  214.1 29.2 all-gather.6
  260.1 149.4 reduce-scatter.6

commit v2 on v0

v2 whole, which is shorter than its diff:
```python
import functools

import jax
import jax.numpy as jnp
from jax import lax
from jax.experimental import pallas as pl
from jax.experimental.pallas import tpu as pltpu
from jax.sharding import PartitionSpec as P

BF = jnp.bfloat16
F32 = jnp.float32
MESH = pl.DeviceIdType.MESH
NX, NZ, NY, NC = 4, 8, 4, 2
TOK, OWN, HALF = 768, 192, 96
COLS, CW, NCH = 1280, 256, 5
FEAT, LROWS, CH = 2048, 32, 384
NT = 4
ORDER = (0, -1, 1, -2, 2, -3, 3, 4)


def body(hid, head_hbm, teach_hbm, labels, temps, mix,
         hgrad, hdgrad,
         hb, hd, ht, part, ra1, rb1, ra2, rb2, ra3, rb3, logit, teach,
         wt, st, r1, r2, ct, coef, grads, hg, ps, pr, zs, zr, ysb, yrb,
         loc_sem, own_sem, ay_s, ay_r, az_s, az_r, ap_s, ap_r,
         rx_s, rx_r, s1_s, s1_r, s2_s, s2_r, gx_s, gx_r,
         pp_s, pp_r, zz_s, zz_r, yy_s, yy_r):
    x = lax.axis_index("dp")
    v = lax.axis_index("vocab")
    c = lax.rem(v, 2)
    y = lax.rem(v // 2, NY)
    z = v // (NY * NC)

    def vid(zz, yy, cc):
        return {"vocab": (zz * NY + yy) * NC + cc}

    def zrel(d):
        return lax.rem(z + (d + NZ), NZ)

    def yrel(d):
        return lax.rem(y + (d + NY), NY)

    def xrel(d):
        return lax.rem(x + (d + NX), NX)

    zup, zdn = vid(zrel(1), y, c), vid(zrel(-1), y, c)
    yup, ydn = vid(z, yrel(1), c), vid(z, yrel(-1), c)
    mate = vid(z, y, 1 - c)
    xup, xdn = {"dp": xrel(1)}, {"dp": xrel(-1)}
    slot = y * NC + c

    def group1(k):
        other = lax.rem(slot + k, 8)
        return vid(z, other // NC, lax.rem(other, NC))

    def group2(k):
        return vid(zrel(k), y, c)

    def rcopy(src, dst, ssem, rsem, dev):
        return pltpu.make_async_remote_copy(
            src_ref=src, dst_ref=dst, send_sem=ssem, recv_sem=rsem,
            device_id=dev, device_id_type=MESH)

    sent = []

    def send(src, dst, ssem, rsem, dev):
        cp = rcopy(src, dst, ssem, rsem, dev)
        cp.start()
        sent.append(cp)
        return cp

    own_copy = pltpu.make_async_copy(hid, hb.at[z, y, c], own_sem)
    own_copy.start()
    head_copies = []
    for j in range(NCH):
        cp = pltpu.make_async_copy(head_hbm.at[:, pl.ds(j * CW, CW)], hd.at[j], loc_sem.at[j])
        cp.start()
        head_copies.append(cp)
    teach_copy = pltpu.make_async_copy(teach_hbm, teach, loc_sem.at[NCH])
    teach_copy.start()

    bar = pltpu.get_barrier_semaphore()
    for k in range(1, 8):
        pl.semaphore_signal(bar, inc=1, device_id=group1(k), device_id_type=MESH)
        pl.semaphore_signal(bar, inc=1, device_id=group2(k), device_id_type=MESH)
    pl.semaphore_signal(bar, inc=1, device_id=xup, device_id_type=MESH)
    pl.semaphore_signal(bar, inc=1, device_id=xdn, device_id_type=MESH)
    pl.semaphore_wait(bar, 16)

    y0 = send(hid, hb.at[z, y, c], ay_s.at[0], ay_r.at[0], yup)
    y1 = send(hid, hb.at[z, y, c], ay_s.at[1], ay_r.at[1], ydn)
    own_copy.wait()
    lo, hi = pl.ds(0, CH), pl.ds(CH, CH)
    y0.wait_recv()
    fw = hb.at[z, yrel(-1), c, :, lo]
    y2 = send(fw, fw, ay_s.at[2], ay_r.at[2], yup)
    y1.wait_recv()
    fw = hb.at[z, yrel(1), c, :, hi]
    y3 = send(fw, fw, ay_s.at[3], ay_r.at[3], ydn)
    y2.wait_recv()
    y3.wait_recv()

    def zsend(d, step):
        up = hb.at[zrel(-d), :, c]
        dn = hb.at[zrel(d), :, c]
        if step < 4:
            return (send(up, up, az_s.at[2 * step - 2], az_r.at[2 * step - 2], zup),
                    send(dn, dn, az_s.at[2 * step - 1], az_r.at[2 * step - 1], zdn))
        up = hb.at[zrel(-d), :, c, :, lo]
        dn = hb.at[zrel(d), :, c, :, hi]
        return (send(up, up, az_s.at[6], az_r.at[6], zup),
                send(dn, dn, az_s.at[7], az_r.at[7], zdn))

    def give(i):
        b = hb.at[zrel(ORDER[i]), :, c]
        return send(b, b, ap_s.at[i], ap_r.at[i], mate)

    gives = [None] * 8
    flights = zsend(0, 1)
    gives[0] = give(0)

    inv = [1.0 / temps[k] for k in range(NT)]
    lane = lax.broadcasted_iota(jnp.int32, (32, 128), 1)
    zeros32 = jnp.zeros((32, 128), F32)

    teach_copy.wait()

    @pl.loop(0, OWN // 32)
    def _(i):
        rows = pl.ds(pl.multiple_of(i * 32, 32), 32)
        t = teach[rows, :].astype(F32)
        m = jnp.max(t, axis=1, keepdims=True)
        t = t - m
        w = jnp.where(lane == 8, m, zeros32)
        for k in range(NT):
            w = jnp.where(lane == 9 + k, jnp.sum(jnp.exp(t * inv[k]), axis=1, keepdims=True), w)
        wt[rows, :] = w

    wt[pl.ds(OWN, 64), :] = jnp.zeros((64, 128), F32)

    for cp in head_copies:
        cp.wait()

    def flip(i):
        blk = hb[zrel(ORDER[i])].reshape(256, TOK)
        ht[i] = blk.T

    def mm(i, j):
        rows = pl.ds(pl.multiple_of(zrel(ORDER[i]) * 256, 256), 256)
        return jnp.dot(ht[i], hd[j, rows, :], preferred_element_type=F32)

    def stage(ids):
        for i in ids:
            gives[i].wait_recv()
            flip(i)

        @pl.loop(0, NCH)
        def _(j):
            acc = mm(ids[0], j)
            for i in ids[1:]:
                acc = acc + mm(i, j)
            if ids[0] != 0:
                acc = acc + part[j]
            part[j] = acc

    done = [0]
    for d in range(1, 5):
        for f in flights:
            f.wait_recv()
        if d < 4:
            flights = zsend(d, d + 1)
            gives[2 * d - 1] = give(2 * d - 1)
            gives[2 * d] = give(2 * d)
        else:
            gives[7] = give(7)
        if d == 1:
            stage([0])
        else:
            stage([2 * d - 3, 2 * d - 2])

    gives[7].wait_recv()
    flip(7)

    def tokens(d, half):
        return pl.ds(pl.multiple_of(xrel(d) * OWN + half * HALF, HALF), HALF)

    def far(j):
        return (rcopy(part.at[j, tokens(2, 0)], ra1.at[j], rx_s.at[0, j], rx_r.at[0, j], xup),
                rcopy(part.at[j, tokens(2, 1)], rb1.at[j], rx_s.at[1, j], rx_r.at[1, j], xdn))

    def near(j):
        return (rcopy(part.at[j, tokens(1, 1)], rb2.at[j], rx_s.at[2, j], rx_r.at[2, j], xup),
                rcopy(part.at[j, tokens(-1, 0)], ra2.at[j], rx_s.at[3, j], rx_r.at[3, j], xdn))

    def relay(j):
        return (rcopy(ra1.at[j], ra3.at[j], rx_s.at[4, j], rx_r.at[4, j], xup),
                rcopy(rb1.at[j], rb3.at[j], rx_s.at[5, j], rx_r.at[5, j], xdn))

    @pl.loop(0, NCH)
    def _(j):
        part[j] = part[j] + mm(7, j)
        for cp in far(j):
            cp.start()

    @pl.loop(0, NCH)
    def _(j):
        for cp in near(j):
            cp.start()

    @pl.loop(0, NCH)
    def _(j):
        fa, fb = far(j)
        r_up, r_dn = relay(j)
        fa.wait_recv()
        ra1[j] = ra1[j] + part[j, tokens(1, 0), :]
        r_up.start()
        fb.wait_recv()
        rb1[j] = rb1[j] + part[j, tokens(-1, 1), :]
        r_dn.start()

    for j in range(NCH):
        nb, na = near(j)
        r_up, r_dn = relay(j)
        na.wait_recv()
        nb.wait_recv()
        r_up.wait_recv()
        r_dn.wait_recv()
        cc = pl.ds(j * CW, CW)
        logit[pl.ds(0, HALF), cc] = part[j, tokens(0, 0), :] + ra2[j] + ra3[j]
        logit[pl.ds(HALF, HALF), cc] = part[j, tokens(0, 1), :] + rb2[j] + rb3[j]

    @pl.loop(0, OWN // 32)
    def _(i):
        rows = pl.ds(pl.multiple_of(i * 32, 32), 32)
        t = logit[rows, :]
        m = jnp.max(t, axis=1, keepdims=True)
        t = t - m
        w = jnp.where(lane == 0, m, wt[rows, :])
        w = jnp.where(lane == 1, jnp.sum(jnp.exp(t), axis=1, keepdims=True), w)
        for k in range(NT):
            w = jnp.where(lane == 2 + k, jnp.sum(jnp.exp(t * inv[k]), axis=1, keepdims=True), w)
        wt[rows, :] = w

    st[0] = wt[...].T[0:16, :]

    def merge(load, n):
        sm = load(0)[0:1, :]
        tm = load(0)[8:9, :]
        for k in range(1, n):
            sm = jnp.maximum(sm, load(k)[0:1, :])
            tm = jnp.maximum(tm, load(k)[8:9, :])
        ss = [0.0] * (1 + NT)
        ts = [0.0] * NT
        for k in range(n):
            s = load(k)
            dm = s[0:1, :] - sm
            dt = s[8:9, :] - tm
            ss[0] = ss[0] + s[1:2, :] * jnp.exp(dm)
            for q in range(NT):
                ss[1 + q] = ss[1 + q] + s[2 + q:3 + q, :] * jnp.exp(dm * inv[q])
                ts[q] = ts[q] + s[9 + q:10 + q, :] * jnp.exp(dt * inv[q])
        return sm, ss, tm, ts

    def exchange(src, dst, ssem, rsem, group):
        flight = [send(src, dst.at[k], ssem.at[k], rsem.at[k], group(k)) for k in range(1, 8)]
        for f in flight:
            f.wait_recv()

    exchange(st.at[0], r1, s1_s, s1_r, group1)
    sm, ss, tm, ts = merge(lambda k: st[0] if k == 0 else r1[k], 8)
    pad = jnp.zeros((2, 256), F32)
    st[1] = jnp.concatenate([sm] + ss + [pad, tm] + ts + [jnp.zeros((3, 256), F32)], axis=0)
    exchange(st.at[1], r2, s2_s, s2_r, group2)
    sm, ss, tm, ts = merge(lambda k: st[1] if k == 0 else r2[k], 8)
    rows = [sm, mix[0] / ss[0]]
    rows += [mix[1] * temps[q] / ss[1 + q] for q in range(NT)]
    rows += [pad, tm]
    rows += [mix[1] * temps[q] / ts[q] for q in range(NT)]
    rows += [jnp.zeros((3, 256), F32)]
    ct[pl.ds(0, 16), :] = jnp.concatenate(rows, axis=0)
    ct[pl.ds(16, 112), :] = jnp.zeros((112, 256), F32)
    coef[...] = ct[...].T

    base = v * COLS
    col = lax.broadcasted_iota(jnp.int32, (32, CW), 1)

    def make_grad(j):
        @pl.loop(0, OWN // 32)
        def _(i):
            rows = pl.ds(pl.multiple_of(i * 32, 32), 32)
            cf = coef[rows, :]
            s = logit[rows, pl.ds(j * CW, CW)] - cf[:, 0:1]
            t = teach[rows, pl.ds(j * CW, CW)].astype(F32) - cf[:, 8:9]
            g = cf[:, 1:2] * jnp.exp(s)
            g = g - jnp.where(col + (base + j * CW) == labels[rows, :], mix[0], 0.0)
            for q in range(NT):
                g = g + cf[:, 2 + q:3 + q] * jnp.exp(s * inv[q])
                g = g - cf[:, 9 + q:10 + q] * jnp.exp(t * inv[q])
            out = pl.ds(pl.multiple_of(x * OWN + i * 32, 32), 32)
            grads[j, out, :] = g.astype(BF)

    def gblock(j, d):
        return grads.at[j, pl.ds(pl.multiple_of(xrel(d) * OWN, OWN), OWN)]

    def gown(j):
        b = gblock(j, 0)
        return (rcopy(b, b, gx_s.at[0, j], gx_r.at[0, j], xup),
                rcopy(b, b, gx_s.at[1, j], gx_r.at[1, j], xdn))

    def gfwd(j):
        a = grads.at[j, tokens(-1, 0)]
        b = grads.at[j, tokens(1, 1)]
        return (rcopy(a, a, gx_s.at[2, j], gx_r.at[2, j], xup),
                rcopy(b, b, gx_s.at[3, j], gx_r.at[3, j], xdn))

    def put(j):
        make_grad(j)
        for cp in gown(j):
            cp.start()

    def passon(j):
        for o, f in zip(gown(j), gfwd(j)):
            o.wait_recv()
            f.start()

    def hidden_part(j, zb):
        rows = pl.ds(pl.multiple_of(zb * 256, 256), 256)
        r = lax.dot_general(hd[j, rows, :], grads[j], (((1,), (1,)), ((), ())),
                            preferred_element_type=F32)
        return r.reshape(NY, NC, LROWS, TOK)

    def head_part(j):
        @pl.loop(0, NZ)
        def _(b):
            lhs = hb[b].reshape(256, TOK)
            r = jnp.dot(lhs, grads[j], preferred_element_type=F32)
            rows = pl.ds(pl.multiple_of(b * 256, 256), 256)
            hdgrad[rows, pl.ds(j * CW, CW)] = r.astype(BF)

    def arrive(j):
        for f in gfwd(j):
            f.wait_recv()

    put(0)
    put(1)
    passon(0)
    for j in range(NCH - 1):
        if j + 2 < NCH:
            put(j + 2)
        passon(j + 1)
        arrive(j)

        @pl.loop(0, NZ)
        def _(b):
            if j == 0:
                hg[b] = hidden_part(j, b)
            else:
                hg[b] = hg[b] + hidden_part(j, b)
        if j > 0:
            head_part(j - 1)
    last = NCH - 1
    arrive(last)

    def pair(i):
        zb = zrel(ORDER[i])
        tot = hg[zb] + hidden_part(last, zb)
        hg[zb] = tot
        ps[i] = hg[zb, :, 1 - c].astype(BF)
        return send(ps.at[i], pr.at[i], pp_s.at[i], pp_r.at[i], mate)

    pairs = {}
    for i in (7, 6, 5, 4, 3, 2, 1, 0):
        pairs[i] = pair(i)

    def total(i):
        pairs[i].wait_recv()
        return hg[zrel(ORDER[i]), :, c] + pr[i].astype(F32)

    def zhop(step, part_id, val, dev):
        zs[step, part_id] = val.astype(BF)
        return send(zs.at[step, part_id], zr.at[step, part_id],
                    zz_s.at[step, part_id], zz_r.at[step, part_id], dev)

    q4 = total(7)
    up_lo = zhop(0, 0, q4[:, :, :CH], zup)
    dn_hi = zhop(0, 3, q4[:, :, CH:], zdn)
    up_hi = dn_lo = None
    for step in range(1, 4):
        dist = 4 - step
        qu = total(2 * dist)
        qd = total(2 * dist - 1)
        nu_hi = qu[:, :, CH:]
        nd_lo = qd[:, :, :CH]
        if up_hi is not None:
            up_hi.wait_recv()
            nu_hi = nu_hi + zr[step - 1, 1].astype(F32)
            dn_lo.wait_recv()
            nd_lo = nd_lo + zr[step - 1, 2].astype(F32)
        up_hi = zhop(step, 1, nu_hi, zup)
        dn_lo = zhop(step, 2, nd_lo, zdn)
        up_lo.wait_recv()
        nu_lo = qu[:, :, :CH] + zr[step - 1, 0].astype(F32)
        up_lo = zhop(step, 0, nu_lo, zup)
        dn_hi.wait_recv()
        nd_hi = qd[:, :, CH:] + zr[step - 1, 3].astype(F32)
        dn_hi = zhop(step, 3, nd_hi, zdn)
        if step < 3:
            head_part(last - 2 + step)

    q0 = total(0)
    up_hi.wait_recv()
    dn_lo.wait_recv()
    up_lo.wait_recv()
    dn_hi.wait_recv()
    own_lo = q0[:, :, :CH] + zr[3, 0].astype(F32) + zr[3, 2].astype(F32)
    own_hi = q0[:, :, CH:] + zr[3, 1].astype(F32) + zr[3, 3].astype(F32)
    ysb[0] = own_lo
    ysb[1] = own_hi

    fa = send(ysb.at[0, yrel(2)], yrb.at[0], yy_s.at[0], yy_r.at[0], yup)
    fb = send(ysb.at[1, yrel(2)], yrb.at[1], yy_s.at[1], yy_r.at[1], ydn)
    nb = send(ysb.at[1, yrel(1)], yrb.at[2], yy_s.at[2], yy_r.at[2], yup)
    na = send(ysb.at[0, yrel(-1)], yrb.at[3], yy_s.at[3], yy_r.at[3], ydn)
    fa.wait_recv()
    yrb[0] = yrb[0] + ysb[0, yrel(1)]
    ga = send(yrb.at[0], yrb.at[4], yy_s.at[4], yy_r.at[4], yup)
    fb.wait_recv()
    yrb[1] = yrb[1] + ysb[1, yrel(-1)]
    gb = send(yrb.at[1], yrb.at[5], yy_s.at[5], yy_r.at[5], ydn)
    na.wait_recv()
    nb.wait_recv()
    ga.wait_recv()
    gb.wait_recv()
    hgrad[:, pl.ds(0, CH)] = ysb[0, y] + yrb[3] + yrb[4]
    hgrad[:, pl.ds(CH, CH)] = ysb[1, y] + yrb[2] + yrb[5]

    for cp in sent:
        cp.wait_send()

    @pl.loop(0, NCH)
    def _(j):
        for cp in far(j) + near(j) + relay(j) + gown(j) + gfwd(j):
            cp.wait_send()


def shards(hidden_t, head, teacher, labels, temps, mix):
    vmem = pl.BlockSpec(memory_space=pltpu.VMEM)
    smem = pl.BlockSpec(memory_space=pltpu.SMEM)
    hbm = pl.BlockSpec(memory_space=pl.ANY)
    dma = pltpu.SemaphoreType.DMA
    half = (NCH, HALF, CW)
    return pl.pallas_call(
        body,
        out_shape=(
            jax.ShapeDtypeStruct((LROWS, TOK), F32),
            jax.ShapeDtypeStruct((FEAT, COLS), BF),
        ),
        in_specs=[vmem, hbm, hbm, vmem, smem, smem],
        out_specs=(vmem, vmem),
        scratch_shapes=[
            pltpu.VMEM((NZ, NY, NC, LROWS, TOK), BF),
            pltpu.VMEM((NCH, FEAT, CW), BF),
            pltpu.VMEM((8, TOK, 256), BF),
            pltpu.VMEM((NCH, TOK, CW), F32),
            pltpu.VMEM(half, F32), pltpu.VMEM(half, F32),
            pltpu.VMEM(half, F32), pltpu.VMEM(half, F32),
            pltpu.VMEM(half, F32), pltpu.VMEM(half, F32),
            pltpu.VMEM((OWN, COLS), F32),
            pltpu.VMEM((OWN, COLS), BF),
            pltpu.VMEM((256, 128), F32),
            pltpu.VMEM((2, 16, 256), F32),
            pltpu.VMEM((8, 16, 256), F32),
            pltpu.VMEM((8, 16, 256), F32),
            pltpu.VMEM((128, 256), F32),
            pltpu.VMEM((256, 128), F32),
            pltpu.VMEM((NCH, TOK, CW), BF),
            pltpu.VMEM((NZ, NY, NC, LROWS, TOK), F32),
            pltpu.VMEM((8, NY, LROWS, TOK), BF),
            pltpu.VMEM((8, NY, LROWS, TOK), BF),
            pltpu.VMEM((4, 4, NY, LROWS, CH), BF),
            pltpu.VMEM((4, 4, NY, LROWS, CH), BF),
            pltpu.VMEM((2, NY, LROWS, CH), F32),
            pltpu.VMEM((6, LROWS, CH), F32),
            dma((NCH + 1,)), dma,
            dma((4,)), dma((4,)),
            dma((8,)), dma((8,)),
            dma((8,)), dma((8,)),
            dma((6, NCH)), dma((6, NCH)),
            dma((8,)), dma((8,)),
            dma((8,)), dma((8,)),
            dma((4, NCH)), dma((4, NCH)),
            dma((8,)), dma((8,)),
            dma((4, 4)), dma((4, 4)),
            dma((6,)), dma((6,)),
        ],
        compiler_params=pltpu.CompilerParams(
            collective_id=0, has_side_effects=True, vmem_limit_bytes=60 * 1024 * 1024
        ),
    )(hidden_t, head, teacher, labels.reshape(OWN, 1), temps, mix)


def solution(mesh):
    placed = (P(("dp", "vocab"), None), P("dp", "vocab"), P("dp", "vocab"), P("dp"), P(), P())
    return jax.shard_map(
        shards,
        mesh=mesh,
        in_specs=placed,
        out_specs=(P(("dp", "vocab"), None), P("dp", "vocab")),
        check_vma=False,
    )
```

time: 862 us -> 157 us (0.18)
  blocking collectives: 497 us -> 0 us
  waiting for transfers between devices: 286 us -> 0 us
  Pallas kernels: 0 us -> 147 us
  matrix products: 29.5 us -> 0 us
  other arithmetic: 13.9 us -> 0 us
  between operations: 13.9 us -> 0.64 us
  local copies, waits for them, and re-layouts: 20.7 us -> 8.16 us
    pmax x1 -> x0, blocking collectives: 251 us -> none  [shards(): highest = lax.pmax(local_peak, 'vocab')]
    psum x1 -> x0, blocking collectives: 246 us -> none  [shards(): lax.psum(jnp.sum(jnp.exp(stacked - highest[:, :, None]), axis=2), 'vocab')]
    pallas_call x0 -> x1, Pallas kernels: none -> 147 us  [shards(): pl.pallas_call(body, out_shape=(jax.ShapeDtypeStruct((LROWS, TOK), F32),...]
    unnamed x5 -> x0, waiting for transfers between devices: 133 us -> none
    all_gather x2 -> x0, waiting for transfers between devices: 111 us -> none  [the longest x1 83.8 us: shards(): h_block = lax.all_gather(hidden_t, 'vocab', axis=0, tiled=True)]
    reduce_scatter x1 -> x0, waiting for transfers between devices: 42.3 us -> none  [shards(): lax.psum_scatter(lax.dot_general(h_block, head, (((0,), (0,)), ((), ())),...]
    dot_general x4 -> x0, matrix products: 29.5 us -> none  [the longest x1 9.99 us: shards(): lax.dot_general(head, grad_all, (((1,), (1,)), ((), ())), preferred_eleme...]
    unnamed x18 -> x2, local copies, waits for them, and re-layouts: 20.1 us -> 6.72 us
  transfers between devices with their start and end apart: 4 -> 0, of which waited for: 4 -> 0; matrix products, arithmetic and copies ran while one was open for 2% -> 0% of each run, Pallas kernels for 0% -> 0%
where the time goes in v2:
time: 157 us; the launch traced here: 156 us
  Pallas kernels  147 us (94%)
  local copies, waits for them, and re-layouts  8.16 us (5%)
    pallas_call x1, Pallas kernels, shards(): pl.pallas_call(body, out_shape=(jax.ShapeDtypeStruct((LROWS, TOK), F32),...  147 us
    unnamed x2, local copies, waits for them, and re-layouts  6.72 us

profile of v2, /device:TPU:2, one launch (start us, length us, event | category | flops | bytes accessed | tf_op | source)
XLA Modules:
  0.0 156.2 jit_solution(17795556680238913605)
XLA Ops:
  0.6 1.4 copy.8.labels
  2.1 147.4 %shard_map.77 = (f32[32,768]{1,0:T(8,128)}, bf16[2048,1280]{1,0:T(8,128)(2,1)}) custom-call(bf16[32,768]{1,0:T(8,128)(2,1)} %hid.1, bf16[2048,1280]{1,0:T(8,128)(2,1)} %head_hbm.1, bf16[192,1280]{1,0:T(8,128)(2,1)} %teach_hbm.1, s32[192,1]{1,0:T(8,128)} %copy.8.labels, f32[4]{0:T(128)} %temps.1, f32[2]{0:T(128)} %mix.1), custom_call_target="tpu_custom_call" | custom-call | tf_op jit(solution)/shard_map/pallas_call | solution.py:452
  149.5 1.5 copy.11
  151.0 5.2 %copy.12 = bf16[2048,1280]{1,0:T(8,128)(2,1)} copy(bf16[2048,1280]{1,0:T(8,128)(2,1)} %get-tuple-element.5) | data formatting | bytes 10485760

commit v3 on v0

v3 whole, which is shorter than its diff:
```python
import jax
import jax.numpy as jnp
from jax import lax
from jax.experimental import pallas as pl
from jax.experimental.pallas import tpu as pltpu
from jax.sharding import PartitionSpec as P

BF = jnp.bfloat16
F32 = jnp.float32
MESH = pl.DeviceIdType.MESH
NX, NZ, NY, NC = 4, 8, 4, 2
TOK, OWN = 768, 192
K = 3
CT = TOK // K
GT = CT // NX
GH = GT // 2
LH = CT // 2
COLS, CW, NCH = 1280, 256, 5
FEAT, LROWS = 2048, 32
NT = 4
ORDER = (0, -1, 1, -2, 2, -3, 3, 4)


def body(hid, head_hbm, teach_hbm, labels, temps, mix,
         hgrad, hdgrad,
         hb, hd, ht, part, ra1, rb1, ra2, rb2, ra3, rb3, logit, teach,
         wt, st, r1, r2, ct, coef, lab, grads, tmp, hgo, ps, pr, zs, zr, ysb, yrb, res,
         loc_sem, ay_s, ay_r, az_s, az_r, ap_s, ap_r,
         rx_s, rx_r, s1_s, s1_r, s2_s, s2_r, gx_s, gx_r,
         pp_s, pp_r, zz_s, zz_r, yy_s, yy_r):
    x = lax.axis_index("dp")
    v = lax.axis_index("vocab")
    c = lax.rem(v, 2)
    y = lax.rem(v // 2, NY)
    z = v // (NY * NC)

    def vid(zz, yy, cc):
        return {"vocab": (zz * NY + yy) * NC + cc}

    def zrel(d):
        return lax.rem(z + (d + NZ), NZ)

    def yrel(d):
        return lax.rem(y + (d + NY), NY)

    def xrel(d):
        return lax.rem(x + (d + NX), NX)

    zup, zdn = vid(zrel(1), y, c), vid(zrel(-1), y, c)
    yup, ydn = vid(z, yrel(1), c), vid(z, yrel(-1), c)
    mate = vid(z, y, 1 - c)
    xup, xdn = {"dp": xrel(1)}, {"dp": xrel(-1)}
    slot = y * NC + c

    def group1(k):
        other = lax.rem(slot + k, 8)
        return vid(z, other // NC, lax.rem(other, NC))

    def group2(k):
        return vid(zrel(k), y, c)

    sent = []

    def send(src, dst, ssem, rsem, dev):
        cp = pltpu.make_async_remote_copy(
            src_ref=src, dst_ref=dst, send_sem=ssem, recv_sem=rsem,
            device_id=dev, device_id_type=MESH)
        cp.start()
        sent.append(cp)
        return cp

    bar = pltpu.get_barrier_semaphore()
    for k in range(1, 8):
        pl.semaphore_signal(bar, inc=1, device_id=group1(k), device_id_type=MESH)
        pl.semaphore_signal(bar, inc=1, device_id=group2(k), device_id_type=MESH)
    pl.semaphore_signal(bar, inc=1, device_id=xup, device_id_type=MESH)
    pl.semaphore_signal(bar, inc=1, device_id=xdn, device_id_type=MESH)

    head_copy = pltpu.make_async_copy(head_hbm, hd, loc_sem.at[0])
    head_copy.start()
    teach_copy = pltpu.make_async_copy(teach_hbm, teach, loc_sem.at[1])
    teach_copy.start()

    h32 = hid[...].astype(F32)
    for k in range(K):
        piece = jnp.concatenate(
            [h32[:, d * OWN + k * GT:d * OWN + (k + 1) * GT] for d in range(NX)], axis=1)
        hb[z, y, c, :, pl.ds(k * CT, CT)] = piece.astype(BF)

    pl.semaphore_wait(bar, 16)

    lo, hi = pl.ds(0, TOK // 2), pl.ds(TOK // 2, TOK // 2)
    own = hb.at[z, y, c]
    y0 = send(own, own, ay_s.at[0], ay_r.at[0], yup)
    y1 = send(own, own, ay_s.at[1], ay_r.at[1], ydn)

    inv = [1.0 / temps[q] for q in range(NT)]
    lane = lax.broadcasted_iota(jnp.int32, (32, 128), 1)
    row3 = lax.broadcasted_iota(jnp.int32, (2, 8, 1), 1)
    blk3 = lax.broadcasted_iota(jnp.int32, (2, 8, 1), 0)
    invc = jnp.zeros((2, 8, 1), F32)
    wcol = jnp.zeros((2, 8, 1), F32)
    invc = jnp.where((blk3 == 0) & (row3 == 1), 1.0, invc)
    wcol = jnp.where((blk3 == 0) & (row3 == 1), mix[0], wcol)
    for q in range(NT):
        hit = ((blk3 == 0) & (row3 == 2 + q)) | ((blk3 == 1) & (row3 == 1 + q))
        invc = jnp.where(hit, inv[q], invc)
        wcol = jnp.where(hit, mix[1] * temps[q], wcol)

    lab[...] = jnp.zeros((256, 128), F32)
    labrow = jnp.concatenate(
        [labels[...].astype(F32), jnp.zeros((1, 256 - OWN), F32)], axis=1)
    lab[...] = jnp.broadcast_to(labrow, (128, 256)).T

    y0.wait_recv()
    fw = hb.at[z, yrel(-1), c, :, lo]
    y2 = send(fw, fw, ay_s.at[2], ay_r.at[2], yup)
    y1.wait_recv()
    fw = hb.at[z, yrel(1), c, :, hi]
    y3 = send(fw, fw, ay_s.at[3], ay_r.at[3], ydn)

    teach_copy.wait()

    def teacher_stats(k):
        @pl.loop(0, GT // 32)
        def _(i):
            r = pl.ds(pl.multiple_of(i * 32, 32), 32)
            t = teach[pl.ds(pl.multiple_of(k * GT + i * 32, 32), 32), :].astype(F32)
            m = jnp.max(t, axis=1, keepdims=True)
            t = t - m
            w = jnp.where(lane == 8, m, 0.0)
            for q in range(NT):
                w = jnp.where(lane == 9 + q, jnp.sum(jnp.exp(t * inv[q]), axis=1, keepdims=True), w)
            wt[k, r, :] = w

        wt[k, pl.ds(GT, 128 - GT), :] = jnp.zeros((128 - GT, 128), F32)

    teacher_stats(0)
    y2.wait_recv()
    y3.wait_recv()

    def zsend(k, d, step):
        ck = pl.ds(k * CT, CT)
        if step < 4:
            up = hb.at[zrel(-d), :, c, :, ck]
            dn = hb.at[zrel(d), :, c, :, ck]
        else:
            up = hb.at[zrel(-d), :, c, :, pl.ds(k * CT, LH)]
            dn = hb.at[zrel(d), :, c, :, pl.ds(k * CT + LH, LH)]
        a, b = 2 * step - 2, 2 * step - 1
        return (send(up, up, az_s.at[k, a], az_r.at[k, a], zup),
                send(dn, dn, az_s.at[k, b], az_r.at[k, b], zdn))

    gives = {}

    def give(k, i):
        b = hb.at[zrel(ORDER[i]), :, c, :, pl.ds(k * CT, CT)]
        gives[k, i] = send(b, b, ap_s.at[k, i], ap_r.at[k, i], mate)

    def stage(k, ids):
        for i in ids:
            gives[k, i].wait_recv()
            blk = hb[zrel(ORDER[i]), :, :, :, pl.ds(k * CT, CT)].reshape(256, CT)
            ht[i] = blk.T

        @pl.loop(0, NCH)
        def _(j):
            cc = pl.ds(pl.multiple_of(j * CW, CW), CW)
            acc = None
            for i in ids:
                rows = pl.ds(pl.multiple_of(zrel(ORDER[i]) * 256, 256), 256)
                t = jnp.dot(ht[i], hd[rows, cc], preferred_element_type=F32)
                acc = t if acc is None else acc + t
            if ids[0] != 0:
                acc = acc + part[k, :, cc]
            part[k, :, cc] = acc

    flights = {}

    def zstart(k):
        flights[k] = zsend(k, 0, 1)
        give(k, 0)

    def advance(k, s):
        for f in flights[k]:
            f.wait_recv()
        if s < 4:
            flights[k] = zsend(k, s, s + 1)
            give(k, 2 * s - 1)
            give(k, 2 * s)
        else:
            give(k, 7)

    STAGES = {1: [0, 1, 2], 2: [3, 4], 3: [5, 6], 4: [7]}

    def tokens(d, half):
        return pl.ds(pl.multiple_of(xrel(d) * GT + half * GH, GH), GH)

    flying = {}

    def far(k):
        flying[k, 0] = send(part.at[k, tokens(2, 0)], ra1.at[k], rx_s.at[k, 0], rx_r.at[k, 0], xup)
        flying[k, 1] = send(part.at[k, tokens(2, 1)], rb1.at[k], rx_s.at[k, 1], rx_r.at[k, 1], xdn)

    def near(k):
        flying[k, 2] = send(part.at[k, tokens(1, 1)], rb2.at[k], rx_s.at[k, 2], rx_r.at[k, 2], xup)
        flying[k, 3] = send(part.at[k, tokens(-1, 0)], ra2.at[k], rx_s.at[k, 3], rx_r.at[k, 3], xdn)

    def relay(k):
        flying[k, 0].wait_recv()
        ra1[k] = ra1[k] + part[k, tokens(1, 0), :]
        flying[k, 4] = send(ra1.at[k], ra3.at[k], rx_s.at[k, 4], rx_r.at[k, 4], xup)
        flying[k, 1].wait_recv()
        rb1[k] = rb1[k] + part[k, tokens(-1, 1), :]
        flying[k, 5] = send(rb1.at[k], rb3.at[k], rx_s.at[k, 5], rx_r.at[k, 5], xdn)

    def final(k):
        for i in (2, 3, 4, 5):
            flying[k, i].wait_recv()
        logit[pl.ds(k * GT, GH), :] = part[k, tokens(0, 0), :] + ra2[k] + ra3[k]
        logit[pl.ds(k * GT + GH, GH), :] = part[k, tokens(0, 1), :] + rb2[k] + rb3[k]

    swaps = {}

    def exchange(k, src, dst, ssem, rsem, group):
        swaps[k] = [send(src, dst.at[k, i], ssem.at[k, i], rsem.at[k, i], group(i))
                    for i in range(1, 8)]

    def local_stats(k):
        @pl.loop(0, GT // 32)
        def _(i):
            r = pl.ds(pl.multiple_of(i * 32, 32), 32)
            t = logit[pl.ds(pl.multiple_of(k * GT + i * 32, 32), 32), :]
            m = jnp.max(t, axis=1, keepdims=True)
            t = t - m
            w = jnp.where(lane == 0, m, wt[k, r, :])
            w = jnp.where(lane == 1, jnp.sum(jnp.exp(t), axis=1, keepdims=True), w)
            for q in range(NT):
                w = jnp.where(lane == 2 + q, jnp.sum(jnp.exp(t * inv[q]), axis=1, keepdims=True), w)
            wt[k, r, :] = w

        st[k, 0] = wt[k].T[0:16, :]
        exchange(k, st.at[k, 0], r1, s1_s, s1_r, group1)

    def merge(k, mine, got):
        for f in swaps[k]:
            f.wait_recv()
        all_s = [st[k, mine].reshape(2, 8, 128)]
        all_s += [got[k, i].reshape(2, 8, 128) for i in range(1, 8)]
        top = all_s[0][:, 0:1, :]
        for s in all_s[1:]:
            top = jnp.maximum(top, s[:, 0:1, :])
        acc = None
        for s in all_s:
            t = s * jnp.exp((s[:, 0:1, :] - top) * invc)
            acc = t if acc is None else acc + t
        return top, acc

    def merge1(k):
        top, acc = merge(k, 0, r1)
        st[k, 1] = jnp.where(row3 == 0, top, acc).reshape(16, 128)
        exchange(k, st.at[k, 1], r2, s2_s, s2_r, group2)

    base = v * COLS
    col = lax.broadcasted_iota(jnp.int32, (32, CW), 1).astype(F32)

    def grad(k):
        top, acc = merge(k, 1, r2)
        acc = jnp.where(wcol > 0.0, acc, 1.0)
        ct[pl.ds(0, 16), :] = jnp.where(row3 == 0, top, wcol / acc).reshape(16, 128)
        ct[pl.ds(16, 112), :] = jnp.zeros((112, 128), F32)
        coef[...] = ct[...].T

        for i in range(GT // 32):
            cf = coef[pl.ds(i * 32, 32), :]
            r = pl.ds(k * GT + i * 32, 32)
            lb = lab[r, 0:1]

            @pl.loop(0, NCH)
            def _(j):
                cc = pl.ds(pl.multiple_of(j * CW, CW), CW)
                s = logit[r, cc] - cf[:, 0:1]
                t = teach[r, cc].astype(F32) - cf[:, 8:9]
                g = cf[:, 1:2] * jnp.exp(s)
                g = g - jnp.where(col + (base + j * CW).astype(F32) == lb, mix[0], 0.0)
                for q in range(NT):
                    g = g + cf[:, 2 + q:3 + q] * jnp.exp(s * inv[q])
                    g = g - cf[:, 9 + q:10 + q] * jnp.exp(t * inv[q])
                out = pl.ds(pl.multiple_of(k * CT + x * GT + i * 32, 32), 32)
                grads[out, cc] = g.astype(BF)

        b = grads.at[pl.ds(pl.multiple_of(k * CT + x * GT, GT), GT)]
        flying[k, 6] = send(b, b, gx_s.at[k, 0], gx_r.at[k, 0], xup)
        flying[k, 7] = send(b, b, gx_s.at[k, 1], gx_r.at[k, 1], xdn)

    def passon(k):
        a = grads.at[pl.ds(pl.multiple_of(k * CT + xrel(-1) * GT, GH), GH)]
        b = grads.at[pl.ds(pl.multiple_of(k * CT + xrel(1) * GT + GH, GH), GH)]
        flying[k, 6].wait_recv()
        flying[k, 8] = send(a, a, gx_s.at[k, 2], gx_r.at[k, 2], xup)
        flying[k, 7].wait_recv()
        flying[k, 9] = send(b, b, gx_s.at[k, 3], gx_r.at[k, 3], xdn)

    pairs = {}

    def pair(k, i):
        zb = zrel(ORDER[i])
        rows = pl.ds(pl.multiple_of(zb * 256, 256), 256)
        r = lax.dot_general(hd[rows, :], grads[pl.ds(k * CT, CT), :], (((1,), (1,)), ((), ())),
                            preferred_element_type=F32)
        tmp[...] = r.reshape(NY, NC, LROWS, CT)
        hgo[k, i] = tmp[:, c]
        ps[k, i] = tmp[:, 1 - c].astype(BF)
        pairs[k, i] = send(ps.at[k, i], pr.at[k, i], pp_s.at[k, i], pp_r.at[k, i], mate)

    def total(k, i):
        pairs[k, i].wait_recv()
        return hgo[k, i] + pr[k, i].astype(F32)

    hops = {}

    def zhop(k, step, lane_id, val, dev):
        zs[k, step, lane_id] = val.astype(BF)
        hops[k, lane_id] = send(zs.at[k, step, lane_id], zr.at[k, step, lane_id],
                                zz_s.at[k, step, lane_id], zz_r.at[k, step, lane_id], dev)

    def got(k, step, lane_id):
        hops[k, lane_id].wait_recv()
        return zr[k, step, lane_id].astype(F32)

    def yhop(k, i, src, dev):
        hops[k, "y", i] = send(src, yrb.at[k, i], yy_s.at[k, i], yy_r.at[k, i], dev)

    def scatter(k, step):
        if step == 0:
            q4 = total(k, 7)
            zhop(k, 0, 0, q4[:, :, :LH], zup)
            zhop(k, 0, 3, q4[:, :, LH:], zdn)
        elif step < 4:
            dist = 4 - step
            qu = total(k, 2 * dist)
            qd = total(k, 2 * dist - 1)
            nu_hi, nd_lo = qu[:, :, LH:], qd[:, :, :LH]
            if step > 1:
                nu_hi = nu_hi + got(k, step - 1, 1)
                nd_lo = nd_lo + got(k, step - 1, 2)
            zhop(k, step, 1, nu_hi, zup)
            zhop(k, step, 2, nd_lo, zdn)
            zhop(k, step, 0, qu[:, :, :LH] + got(k, step - 1, 0), zup)
            zhop(k, step, 3, qd[:, :, LH:] + got(k, step - 1, 3), zdn)
        elif step == 4:
            q0 = total(k, 0)
            ysb[k, 0] = q0[:, :, :LH] + got(k, 3, 0) + got(k, 3, 2)
            ysb[k, 1] = q0[:, :, LH:] + got(k, 3, 1) + got(k, 3, 3)
            yhop(k, 0, ysb.at[k, 0, yrel(2)], yup)
            yhop(k, 1, ysb.at[k, 1, yrel(2)], ydn)
            yhop(k, 2, ysb.at[k, 1, yrel(1)], yup)
            yhop(k, 3, ysb.at[k, 0, yrel(-1)], ydn)
        elif step == 5:
            hops[k, "y", 0].wait_recv()
            yrb[k, 0] = yrb[k, 0] + ysb[k, 0, yrel(1)]
            yhop(k, 4, yrb.at[k, 0], yup)
            hops[k, "y", 1].wait_recv()
            yrb[k, 1] = yrb[k, 1] + ysb[k, 1, yrel(-1)]
            yhop(k, 5, yrb.at[k, 1], ydn)
        else:
            for i in (2, 3, 4, 5):
                hops[k, "y", i].wait_recv()
            res[k, :, pl.ds(0, LH)] = ysb[k, 0, y] + yrb[k, 3] + yrb[k, 4]
            res[k, :, pl.ds(LH, LH)] = ysb[k, 1, y] + yrb[k, 2] + yrb[k, 5]

    def head_part(b):
        lhs = hb[b].reshape(256, TOK)

        @pl.loop(0, NCH)
        def _(j):
            cc = pl.ds(pl.multiple_of(j * CW, CW), CW)
            r = jnp.dot(lhs, grads[:, cc], preferred_element_type=F32)
            hdgrad[pl.ds(b * 256, 256), cc] = r.astype(BF)

    zstart(0)
    teacher_stats(1)
    head_copy.wait()
    for t in range(8):
        for k in range(K):
            s = t - 2 * k + 1
            if 1 <= s <= 4:
                advance(k, s)
        if t in (1, 3):
            zstart((t + 1) // 2)
        for k in range(K):
            s = t - 2 * k + 1
            if 1 <= s <= 4:
                stage(k, STAGES[s])
                if s == 4:
                    far(k)
                    if k > 0:
                        relay(k - 1)
                    near(k)
        if t == 2:
            teacher_stats(2)

    final(0)
    local_stats(0)
    merge1(0)
    relay(2)
    final(1)
    local_stats(1)
    grad(0)
    merge1(1)
    final(2)
    local_stats(2)
    grad(1)
    passon(0)
    merge1(2)
    passon(1)
    for i in (8, 9):
        flying[0, i].wait_recv()
    for i in (7, 6, 5, 4):
        pair(0, i)
    grad(2)
    for i in (3, 2, 1, 0):
        pair(0, i)
    scatter(0, 0)
    for i in (8, 9):
        flying[1, i].wait_recv()
    passon(2)
    for i in (7, 6, 5, 4):
        pair(1, i)
    scatter(0, 1)
    for i in (3, 2, 1, 0):
        pair(1, i)
    scatter(1, 0)
    for i in (8, 9):
        flying[2, i].wait_recv()
    pair(2, 7)
    pair(2, 6)
    pair(2, 5)
    scatter(2, 0)
    for i in (4, 3, 2, 1, 0):
        pair(2, i)
    scatter(1, 1)
    scatter(0, 2)
    for t in range(1, 7):
        scatter(2, t)
        if t + 1 < 7:
            scatter(1, t + 1)
        if t + 2 < 7:
            scatter(0, t + 2)
        for b in {1: (0, 1), 2: (2, 3), 3: (4, 5), 4: (6,), 5: (7,)}.get(t, ()):
            head_part(b)

    full = [res[k] for k in range(K)]
    hgrad[...] = jnp.concatenate(
        [full[k][:, d * GT:(d + 1) * GT] for d in range(NX) for k in range(K)], axis=1)

    for cp in sent:
        cp.wait_send()


def shards(hidden_t, head, teacher, labels, temps, mix):
    vmem = pl.BlockSpec(memory_space=pltpu.VMEM)
    smem = pl.BlockSpec(memory_space=pltpu.SMEM)
    hbm = pl.BlockSpec(memory_space=pl.ANY)
    dma = pltpu.SemaphoreType.DMA
    half = (K, GH, COLS)
    return pl.pallas_call(
        body,
        out_shape=(
            jax.ShapeDtypeStruct((LROWS, TOK), F32),
            jax.ShapeDtypeStruct((FEAT, COLS), BF),
        ),
        in_specs=[vmem, hbm, hbm, vmem, smem, smem],
        out_specs=(vmem, vmem),
        scratch_shapes=[
            pltpu.VMEM((NZ, NY, NC, LROWS, TOK), BF),
            pltpu.VMEM((FEAT, COLS), BF),
            pltpu.VMEM((8, CT, 256), BF),
            pltpu.VMEM((K, CT, COLS), F32),
            pltpu.VMEM(half, F32), pltpu.VMEM(half, F32),
            pltpu.VMEM(half, F32), pltpu.VMEM(half, F32),
            pltpu.VMEM(half, F32), pltpu.VMEM(half, F32),
            pltpu.VMEM((OWN, COLS), F32),
            pltpu.VMEM((OWN, COLS), BF),
            pltpu.VMEM((K, 128, 128), F32),
            pltpu.VMEM((K, 2, 16, 128), F32),
            pltpu.VMEM((K, 8, 16, 128), F32),
            pltpu.VMEM((K, 8, 16, 128), F32),
            pltpu.VMEM((128, 128), F32),
            pltpu.VMEM((128, 128), F32),
            pltpu.VMEM((256, 128), F32),
            pltpu.VMEM((TOK, COLS), BF),
            pltpu.VMEM((NY, NC, LROWS, CT), F32),
            pltpu.VMEM((K, 8, NY, LROWS, CT), F32),
            pltpu.VMEM((K, 8, NY, LROWS, CT), BF),
            pltpu.VMEM((K, 8, NY, LROWS, CT), BF),
            pltpu.VMEM((K, 4, 4, NY, LROWS, LH), BF),
            pltpu.VMEM((K, 4, 4, NY, LROWS, LH), BF),
            pltpu.VMEM((K, 2, NY, LROWS, LH), F32),
            pltpu.VMEM((K, 6, LROWS, LH), F32),
            pltpu.VMEM((K, LROWS, CT), F32),
            dma((2,)),
            dma((4,)), dma((4,)),
            dma((K, 8)), dma((K, 8)),
            dma((K, 8)), dma((K, 8)),
            dma((K, 6)), dma((K, 6)),
            dma((K, 8)), dma((K, 8)),
            dma((K, 8)), dma((K, 8)),
            dma((K, 4)), dma((K, 4)),
            dma((K, 8)), dma((K, 8)),
            dma((K, 4, 4)), dma((K, 4, 4)),
            dma((K, 6)), dma((K, 6)),
        ],
        compiler_params=pltpu.CompilerParams(
            collective_id=0, has_side_effects=True, vmem_limit_bytes=56 * 1024 * 1024
        ),
    )(hidden_t, head, teacher, labels.reshape(1, OWN), temps, mix)


def solution(mesh):
    placed = (P(("dp", "vocab"), None), P("dp", "vocab"), P("dp", "vocab"), P("dp"), P(), P())
    return jax.shard_map(
        shards,
        mesh=mesh,
        in_specs=placed,
        out_specs=(P(("dp", "vocab"), None), P("dp", "vocab")),
        check_vma=False,
    )
```

time: 862 us -> 138 us (0.16)
  blocking collectives: 497 us -> 0 us
  waiting for transfers between devices: 286 us -> 0 us
  Pallas kernels: 0 us -> 129 us
  matrix products: 29.5 us -> 0 us
  local copies, waits for them, and re-layouts: 20.7 us -> 6.72 us
  other arithmetic: 13.9 us -> 0 us
  between operations: 13.9 us -> 0.64 us
    pmax x1 -> x0, blocking collectives: 251 us -> none  [shards(): highest = lax.pmax(local_peak, 'vocab')]
    psum x1 -> x0, blocking collectives: 246 us -> none  [shards(): lax.psum(jnp.sum(jnp.exp(stacked - highest[:, :, None]), axis=2), 'vocab')]
    unnamed x5 -> x0, waiting for transfers between devices: 133 us -> none
    pallas_call x0 -> x1, Pallas kernels: none -> 129 us  [shards(): pl.pallas_call(body, out_shape=(jax.ShapeDtypeStruct((LROWS, TOK), F32),...]
    all_gather x2 -> x0, waiting for transfers between devices: 111 us -> none  [the longest x1 83.8 us: shards(): h_block = lax.all_gather(hidden_t, 'vocab', axis=0, tiled=True)]
    reduce_scatter x1 -> x0, waiting for transfers between devices: 42.3 us -> none  [shards(): lax.psum_scatter(lax.dot_general(h_block, head, (((0,), (0,)), ((), ())),...]
    dot_general x4 -> x0, matrix products: 29.5 us -> none  [the longest x1 9.99 us: shards(): lax.dot_general(head, grad_all, (((1,), (1,)), ((), ())), preferred_eleme...]
    unnamed x18 -> x2, local copies, waits for them, and re-layouts: 20.1 us -> 6.72 us
  transfers between devices with their start and end apart: 4 -> 0, of which waited for: 4 -> 0; matrix products, arithmetic and copies ran while one was open for 2% -> 0% of each run, Pallas kernels for 0% -> 0%
where the time goes in v3:
time: 138 us; the launch traced here: 137 us
  Pallas kernels  129 us (93%)
  local copies, waits for them, and re-layouts  6.72 us (5%)
    pallas_call x1, Pallas kernels, shards(): pl.pallas_call(body, out_shape=(jax.ShapeDtypeStruct((LROWS, TOK), F32),...  129 us
    unnamed x2, local copies, waits for them, and re-layouts  6.72 us

profile of v3, /device:TPU:2, one launch (start us, length us, event | category | flops | bytes accessed | tf_op | source)
XLA Modules:
  0.0 136.5 jit_solution(829239868647308588)
XLA Ops:
  0.6 129.2 %shard_map.77 = (f32[32,768]{1,0:T(8,128)}, bf16[2048,1280]{1,0:T(8,128)(2,1)}) custom-call(bf16[32,768]{1,0:T(8,128)(2,1)} %hid.1, bf16[2048,1280]{1,0:T(8,128)(2,1)} %head_hbm.1, bf16[192,1280]{1,0:T(8,128)(2,1)} %teach_hbm.1, s32[1,192]{1,0:T(1,128)} %bitcast.1, f32[4]{0:T(128)} %temps.1, f32[2]{0:T(128)} %mix.1), custom_call_target="tpu_custom_call" | custom-call | tf_op jit(solution)/shard_map/pallas_call | solution.py:467
  129.8 1.5 %copy.10 = f32[32,768]{1,0:T(8,128)} copy(f32[32,768]{1,0:T(8,128)} %get-tuple-element.4) | data formatting | bytes 196608
  131.3 5.2 %copy.11 = bf16[2048,1280]{1,0:T(8,128)(2,1)} copy(bf16[2048,1280]{1,0:T(8,128)(2,1)} %get-tuple-element.5) | data formatting | bytes 10485760

commit v4 on v3

v4 whole, which is shorter than its diff:
```python
import jax
import jax.numpy as jnp
from jax import lax
from jax.experimental import pallas as pl
from jax.experimental.pallas import tpu as pltpu
from jax.sharding import PartitionSpec as P

BF = jnp.bfloat16
F32 = jnp.float32
MESH = pl.DeviceIdType.MESH
NX, NZ, NY, NC = 4, 8, 4, 2
TOK, OWN = 768, 192
K = 3
CT = TOK // K
GT = CT // NX
GH = GT // 2
LH = CT // 2
COLS, CW, NCH = 1280, 256, 5
FEAT, LROWS = 2048, 32
NT = 4
GATHER = (0, -1, 1, 2)
SPREAD = (2, 1, -1, 0)


def body(hid_hbm, head_hbm, teach_hbm, labels_hbm, temps_hbm, mix_hbm,
         hgrad, hdgrad,
         hid, labels, temps, mix, hdo,
         hb, hd, ht, part, ra1, rb1, ra2, rb2, ra3, rb3, logit, teach,
         wt, st, r1, r2, ct, coef, lab, grads, tmp, hgo, ps, pr, ysb, yrb, ysum, zsb, zrb, res,
         loc_sem, out_sem, fy_s, fy_r, ay_s, ay_r, az_s, az_r, ap_s, ap_r,
         rx_s, rx_r, s1_s, s1_r, s2_s, s2_r, gx_s, gx_r,
         pp_s, pp_r, zz_s, zz_r, yy_s, yy_r):
    x = lax.axis_index("dp")
    v = lax.axis_index("vocab")
    c = lax.rem(v, 2)
    y = lax.rem(v // 2, NY)
    z = v // (NY * NC)

    def vid(zz, yy, cc):
        return {"vocab": (zz * NY + yy) * NC + cc}

    def zrel(d):
        return lax.rem(z + (d + NZ), NZ)

    def yrel(d):
        return lax.rem(y + (d + NY), NY)

    def xrel(d):
        return lax.rem(x + (d + NX), NX)

    yup, ydn = vid(z, yrel(1), c), vid(z, yrel(-1), c)
    mate = vid(z, y, 1 - c)
    xup, xdn = {"dp": xrel(1)}, {"dp": xrel(-1)}
    slot = y * NC + c

    def group1(k):
        other = lax.rem(slot + k, 8)
        return vid(z, other // NC, lax.rem(other, NC))

    def group2(k):
        return vid(zrel(k), y, c)

    sent = []

    def send(src, dst, ssem, rsem, dev):
        cp = pltpu.make_async_remote_copy(
            src_ref=src, dst_ref=dst, send_sem=ssem, recv_sem=rsem,
            device_id=dev, device_id_type=MESH)
        cp.start()
        sent.append(cp)
        return cp

    small = []
    for n, (a, b) in enumerate(((hid_hbm, hid), (labels_hbm, labels), (temps_hbm, temps), (mix_hbm, mix))):
        cp = pltpu.make_async_copy(a, b, loc_sem.at[2 + n])
        cp.start()
        small.append(cp)

    bar = pltpu.get_barrier_semaphore()
    for k in range(4, 0, -1):
        for i in {4: (4,)}.get(k, (k, NZ - k)):
            pl.semaphore_signal(bar, inc=1, device_id=group2(i), device_id_type=MESH)
    for k in range(1, 8):
        pl.semaphore_signal(bar, inc=1, device_id=group1(k), device_id_type=MESH)
    pl.semaphore_signal(bar, inc=1, device_id=xup, device_id_type=MESH)
    pl.semaphore_signal(bar, inc=1, device_id=xdn, device_id_type=MESH)

    head_copy = pltpu.make_async_copy(head_hbm, hd, loc_sem.at[0])
    head_copy.start()
    teach_copy = pltpu.make_async_copy(teach_hbm, teach, loc_sem.at[1])
    teach_copy.start()

    for cp in small:
        cp.wait()

    h32 = hid[...].astype(F32)
    for k in range(K):
        piece = jnp.concatenate(
            [h32[:, d * OWN + k * GT:d * OWN + (k + 1) * GT] for d in range(NX)], axis=1)
        hb[k, z, y, c] = piece.astype(BF)

    pl.semaphore_wait(bar, 16)

    zin = {}
    fin = {}

    def zsend(k):
        own = hb.at[k, z, y, c]
        for i in range(1, NZ):
            zin[k, i] = send(own, own, az_s.at[k, i], az_r.at[k, i], group2(i))

    def piece_out(i):
        b = hb.at[0, zrel(-i), y, c]
        fin[i, 0] = send(b, b, fy_s.at[i, 0], fy_r.at[i, 0], yup)
        fin[i, 1] = send(b, b, fy_s.at[i, 1], fy_r.at[i, 1], ydn)

    def piece_on(i):
        fin[i, 0].wait_recv()
        b = hb.at[0, zrel(-i), yrel(-1), c, :, pl.ds(0, LH)]
        fin[i, 2] = send(b, b, fy_s.at[i, 2], fy_r.at[i, 2], yup)
        fin[i, 1].wait_recv()
        b = hb.at[0, zrel(-i), yrel(1), c, :, pl.ds(LH, LH)]
        fin[i, 3] = send(b, b, fy_s.at[i, 3], fy_r.at[i, 3], ydn)

    zsend(0)
    piece_out(0)

    inv = [1.0 / temps[q] for q in range(NT)]
    lane = lax.broadcasted_iota(jnp.int32, (32, 128), 1)
    row2 = lax.broadcasted_iota(jnp.int32, (8, 128), 0)
    left = lax.broadcasted_iota(jnp.int32, (8, 128), 1) < 64
    invc = jnp.where(left & (row2 == 1), 1.0, 0.0)
    wcol = jnp.where(left & (row2 == 1), mix[0], 0.0)
    for q in range(NT):
        hit = (left & (row2 == 2 + q)) | (jnp.logical_not(left) & (row2 == 1 + q))
        invc = jnp.where(hit, inv[q], invc)
        wcol = jnp.where(hit, mix[1] * temps[q], wcol)

    lab[...] = jnp.zeros((256, 128), F32)
    labrow = jnp.concatenate(
        [labels[...].astype(F32), jnp.zeros((1, 256 - OWN), F32)], axis=1)
    lab[...] = jnp.broadcast_to(labrow, (128, 256)).T

    teach_copy.wait()

    def teacher_stats(k):
        @pl.loop(0, GT // 32)
        def _(i):
            r = pl.ds(pl.multiple_of(i * 32, 32), 32)
            t = teach[pl.ds(pl.multiple_of(k * GT + i * 32, 32), 32), :].astype(F32)
            m = jnp.max(t, axis=1, keepdims=True)
            t = t - m
            w = jnp.where(lane == 8, m, 0.0)
            for q in range(NT):
                w = jnp.where(lane == 9 + q, jnp.sum(jnp.exp(t * inv[q]), axis=1, keepdims=True), w)
            wt[k, r, :] = w

        wt[k, pl.ds(GT, 128 - GT), :] = jnp.zeros((128 - GT, 128), F32)

    teacher_stats(0)

    yin = {}
    gives = {}

    def bundle(k, d):
        return hb.at[k, :, yrel(d), c]

    def give(k, i):
        b = bundle(k, GATHER[i])
        gives[k, i] = send(b, b, ap_s.at[k, i], ap_r.at[k, i], mate)

    def yfirst(k):
        for i in range(1, NZ):
            zin[k, i].wait_recv()
        b = bundle(k, 0)
        yin[k, 0] = send(b, b, ay_s.at[k, 0], ay_r.at[k, 0], yup)
        yin[k, 1] = send(b, b, ay_s.at[k, 1], ay_r.at[k, 1], ydn)
        give(k, 0)

    def ysecond(k):
        yin[k, 0].wait_recv()
        b = hb.at[k, :, yrel(-1), c, :, pl.ds(0, LH)]
        yin[k, 2] = send(b, b, ay_s.at[k, 2], ay_r.at[k, 2], yup)
        yin[k, 1].wait_recv()
        b = hb.at[k, :, yrel(1), c, :, pl.ds(LH, LH)]
        yin[k, 3] = send(b, b, ay_s.at[k, 3], ay_r.at[k, 3], ydn)
        give(k, 1)
        give(k, 2)

    def ythird(k):
        yin[k, 2].wait_recv()
        yin[k, 3].wait_recv()
        give(k, 3)

    def stage(k, i):
        gives[k, i].wait_recv()
        yb = yrel(GATHER[i])
        ht[...] = hb[k, :, yb].reshape(512, CT).T

        for j in range(NCH):
            cc = pl.ds(j * CW, CW)
            acc = jnp.dot(ht[...], hd[:, yb, :, cc].reshape(512, CW), preferred_element_type=F32)
            if i != 0:
                acc = acc + part[k, :, cc]
            part[k, :, cc] = acc

    def tokens(d, half):
        return pl.ds(pl.multiple_of(xrel(d) * GT + half * GH, GH), GH)

    flying = {}

    def far(k):
        flying[k, 0] = send(part.at[k, tokens(2, 0)], ra1.at[k], rx_s.at[k, 0], rx_r.at[k, 0], xup)
        flying[k, 1] = send(part.at[k, tokens(2, 1)], rb1.at[k], rx_s.at[k, 1], rx_r.at[k, 1], xdn)

    def near(k):
        flying[k, 2] = send(part.at[k, tokens(1, 1)], rb2.at[k], rx_s.at[k, 2], rx_r.at[k, 2], xup)
        flying[k, 3] = send(part.at[k, tokens(-1, 0)], ra2.at[k], rx_s.at[k, 3], rx_r.at[k, 3], xdn)

    def relay(k):
        flying[k, 0].wait_recv()
        ra1[k] = ra1[k] + part[k, tokens(1, 0), :]
        flying[k, 4] = send(ra1.at[k], ra3.at[k], rx_s.at[k, 4], rx_r.at[k, 4], xup)
        flying[k, 1].wait_recv()
        rb1[k] = rb1[k] + part[k, tokens(-1, 1), :]
        flying[k, 5] = send(rb1.at[k], rb3.at[k], rx_s.at[k, 5], rx_r.at[k, 5], xdn)

    def final(k):
        for i in (2, 3, 4, 5):
            flying[k, i].wait_recv()
        logit[pl.ds(k * GT, GH), :] = part[k, tokens(0, 0), :] + ra2[k] + ra3[k]
        logit[pl.ds(k * GT + GH, GH), :] = part[k, tokens(0, 1), :] + rb2[k] + rb3[k]

    swaps = {}

    def exchange(k, src, dst, ssem, rsem, group):
        swaps[k] = [send(src, dst.at[k, i], ssem.at[k, i], rsem.at[k, i], group(i))
                    for i in range(1, 8)]

    def local_stats(k):
        @pl.loop(0, GT // 32)
        def _(i):
            r = pl.ds(pl.multiple_of(i * 32, 32), 32)
            t = logit[pl.ds(pl.multiple_of(k * GT + i * 32, 32), 32), :]
            m = jnp.max(t, axis=1, keepdims=True)
            t = t - m
            w = jnp.where(lane == 0, m, wt[k, r, :])
            w = jnp.where(lane == 1, jnp.sum(jnp.exp(t), axis=1, keepdims=True), w)
            for q in range(NT):
                w = jnp.where(lane == 2 + q, jnp.sum(jnp.exp(t * inv[q]), axis=1, keepdims=True), w)
            wt[k, r, :] = w

        flat = wt[k].T
        st[k, 0] = jnp.where(left, flat[0:8, :], pltpu.roll(flat[8:16, :], 64, 1))
        exchange(k, st.at[k, 0], r1, s1_s, s1_r, group1)

    def merge(k, mine, got):
        for f in swaps[k]:
            f.wait_recv()
        all_s = [st[k, mine]] + [got[k, i] for i in range(1, 8)]
        top = all_s[0][0:1, :]
        for s in all_s[1:]:
            top = jnp.maximum(top, s[0:1, :])
        acc = None
        for s in all_s:
            t = s * jnp.exp((s[0:1, :] - top) * invc)
            acc = t if acc is None else acc + t
        return top, acc

    def merge1(k):
        top, acc = merge(k, 0, r1)
        st[k, 1] = jnp.where(row2 == 0, top, acc)
        exchange(k, st.at[k, 1], r2, s2_s, s2_r, group2)

    base = v * COLS
    col = lax.broadcasted_iota(jnp.int32, (32, CW), 1).astype(F32)

    def grad(k):
        top, acc = merge(k, 1, r2)
        acc = jnp.where(wcol > 0.0, acc, 1.0)
        both = jnp.where(row2 == 0, top, wcol / acc)
        ct[pl.ds(0, 8), :] = both
        ct[pl.ds(8, 8), :] = pltpu.roll(both, 64, 1)
        ct[pl.ds(16, 112), :] = jnp.zeros((112, 128), F32)
        coef[...] = ct[...].T

        for i in range(GT // 32):
            cf = coef[pl.ds(i * 32, 32), :]
            r = pl.ds(k * GT + i * 32, 32)
            lb = lab[r, 0:1]

            @pl.loop(0, NCH)
            def _(j):
                cc = pl.ds(pl.multiple_of(j * CW, CW), CW)
                s = logit[r, cc] - cf[:, 0:1]
                t = teach[r, cc].astype(F32) - cf[:, 8:9]
                g = cf[:, 1:2] * jnp.exp(s)
                g = g - jnp.where(col + (base + j * CW).astype(F32) == lb, mix[0], 0.0)
                for q in range(NT):
                    g = g + cf[:, 2 + q:3 + q] * jnp.exp(s * inv[q])
                    g = g - cf[:, 9 + q:10 + q] * jnp.exp(t * inv[q])
                out = pl.ds(pl.multiple_of(k * CT + x * GT + i * 32, 32), 32)
                grads[out, cc] = g.astype(BF)

        b = grads.at[pl.ds(pl.multiple_of(k * CT + x * GT, GT), GT)]
        flying[k, 6] = send(b, b, gx_s.at[k, 0], gx_r.at[k, 0], xup)
        flying[k, 7] = send(b, b, gx_s.at[k, 1], gx_r.at[k, 1], xdn)

    def passon(k):
        a = grads.at[pl.ds(pl.multiple_of(k * CT + xrel(-1) * GT, GH), GH)]
        b = grads.at[pl.ds(pl.multiple_of(k * CT + xrel(1) * GT + GH, GH), GH)]
        flying[k, 6].wait_recv()
        flying[k, 8] = send(a, a, gx_s.at[k, 2], gx_r.at[k, 2], xup)
        flying[k, 7].wait_recv()
        flying[k, 9] = send(b, b, gx_s.at[k, 3], gx_r.at[k, 3], xdn)

    def landed(k):
        for i in (8, 9):
            flying[k, i].wait_recv()

    pairs = {}

    def pair(k, i):
        yb = yrel(SPREAD[i])
        r = lax.dot_general(hd[:, yb].reshape(512, COLS), grads[pl.ds(k * CT, CT), :],
                            (((1,), (1,)), ((), ())), preferred_element_type=F32)
        tmp[...] = r.reshape(NZ, NC, LROWS, CT)
        hgo[k, i] = tmp[:, c]
        ps[k, i] = tmp[:, 1 - c].astype(BF)
        pairs[k, i] = send(ps.at[k, i], pr.at[k, i], pp_s.at[k, i], pp_r.at[k, i], mate)

    LO, HI = pl.ds(0, LH), pl.ds(LH, LH)

    def total(k, i, part_of):
        return hgo[k, i, :, :, part_of] + pr[k, i, :, :, part_of].astype(F32)

    hops = {}

    def yhop(k, i, val, dev):
        ysb[k, i] = val.astype(BF)
        hops[k, i] = send(ysb.at[k, i], yrb.at[k, i], yy_s.at[k, i], yy_r.at[k, i], dev)

    def scatter(k, step):
        if step == 0:
            pairs[k, 0].wait_recv()
            yhop(k, 0, total(k, 0, LO), yup)
            yhop(k, 1, total(k, 0, HI), ydn)
        elif step == 1:
            pairs[k, 1].wait_recv()
            yhop(k, 2, total(k, 1, HI), yup)
            pairs[k, 2].wait_recv()
            yhop(k, 3, total(k, 2, LO), ydn)
        elif step == 2:
            hops[k, 0].wait_recv()
            yhop(k, 4, total(k, 1, LO) + yrb[k, 0].astype(F32), yup)
            hops[k, 1].wait_recv()
            yhop(k, 5, total(k, 2, HI) + yrb[k, 1].astype(F32), ydn)
        elif step == 3:
            pairs[k, 3].wait_recv()
            for i in (2, 3, 4, 5):
                hops[k, i].wait_recv()
            ysum[:, :, LO] = total(k, 3, LO) + yrb[k, 3].astype(F32) + yrb[k, 4].astype(F32)
            ysum[:, :, HI] = total(k, 3, HI) + yrb[k, 2].astype(F32) + yrb[k, 5].astype(F32)
            zsb[k] = ysum[...].astype(BF)
            res[k] = ysum[z]
            for i in range(1, NZ):
                hops[k, "z", i] = send(zsb.at[k, zrel(i)], zrb.at[k, i],
                                       zz_s.at[k, i], zz_r.at[k, i], group2(i))
        else:
            for i in range(1, NZ):
                hops[k, "z", i].wait_recv()
            acc = res[k]
            for i in range(1, NZ):
                acc = acc + zrb[k, i].astype(F32)
            res[k] = acc

    outs = []

    def head_part(b):
        for j in range(NCH):
            cc = pl.ds(j * CW, CW)
            r = None
            for k in range(K):
                t = jnp.dot(hb[k, b].reshape(256, CT), grads[pl.ds(k * CT, CT), cc],
                            preferred_element_type=F32)
                r = t if r is None else r + t
            hdo[pl.ds(b * 256, 256), cc] = r.astype(BF)
        rows = pl.ds(b * 256, 256)
        outs.append(pltpu.make_async_copy(hdo.at[rows], hdgrad.at[rows], out_sem.at[b]))
        outs[-1].start()

    NEAREST = (1, 7, 2, 6, 3, 5, 4)
    for i in NEAREST:
        zin[0, i].wait_recv()
        piece_out(i)
    give(0, 0)
    zsend(1)
    for i in (0,) + NEAREST:
        piece_on(i)
    give(0, 1)
    give(0, 2)
    zsend(2)
    head_copy.wait()
    stage(0, 0)
    yfirst(1)
    stage(0, 1)
    stage(0, 2)
    for i in (0,) + NEAREST:
        fin[i, 2].wait_recv()
        fin[i, 3].wait_recv()
    give(0, 3)
    stage(0, 3)
    far(0)
    near(0)
    ysecond(1)
    teacher_stats(1)
    stage(1, 0)
    yfirst(2)
    stage(1, 1)
    stage(1, 2)
    ythird(1)
    relay(0)
    stage(1, 3)
    far(1)
    near(1)
    teacher_stats(2)
    ysecond(2)
    stage(2, 0)
    stage(2, 1)
    stage(2, 2)
    ythird(2)
    final(0)
    local_stats(0)
    stage(2, 3)
    far(2)
    relay(1)
    near(2)
    merge1(0)
    relay(2)
    grad(0)
    final(1)
    local_stats(1)
    merge1(1)
    final(2)
    local_stats(2)
    passon(0)
    merge1(2)
    grad(1)
    landed(0)
    pair(0, 0)
    pair(0, 1)
    scatter(0, 0)
    passon(1)
    grad(2)
    pair(0, 2)
    pair(0, 3)
    scatter(0, 1)
    scatter(0, 2)
    landed(1)
    pair(1, 0)
    pair(1, 1)
    scatter(1, 0)
    passon(2)
    scatter(0, 3)
    pair(1, 2)
    pair(1, 3)
    scatter(1, 1)
    landed(2)
    pair(2, 0)
    scatter(1, 2)
    pair(2, 1)
    pair(2, 2)
    scatter(2, 0)
    pair(2, 3)
    scatter(1, 3)
    scatter(2, 1)
    head_part(0)
    head_part(1)
    scatter(2, 2)
    head_part(2)
    head_part(3)
    head_part(4)
    scatter(2, 3)
    for b in (5, 6, 7):
        head_part(b)
    scatter(0, 4)
    scatter(1, 4)
    scatter(2, 4)

    full = [res[k] for k in range(K)]
    hgrad[...] = jnp.concatenate(
        [full[k][:, d * GT:(d + 1) * GT] for d in range(NX) for k in range(K)], axis=1)

    for cp in sent:
        cp.wait_send()
    for cp in outs:
        cp.wait()


def shards(hidden_t, head, teacher, labels, temps, mix):
    vmem = pl.BlockSpec(memory_space=pltpu.VMEM)
    hbm = pl.BlockSpec(memory_space=pl.ANY)
    dma = pltpu.SemaphoreType.DMA
    half = (K, GH, COLS)
    return pl.pallas_call(
        body,
        out_shape=(
            pltpu.VMEM((LROWS, TOK), F32),
            pltpu.VMEM((FEAT, COLS), BF),
        ),
        in_specs=[hbm] * 6,
        out_specs=(vmem, hbm),
        scratch_shapes=[
            pltpu.VMEM((LROWS, TOK), BF),
            pltpu.VMEM((1, OWN), jnp.int32),
            pltpu.SMEM((NT,), F32),
            pltpu.SMEM((2,), F32),
            pltpu.VMEM((FEAT, COLS), BF),
            pltpu.VMEM((K, NZ, NY, NC, LROWS, CT), BF),
            pltpu.VMEM((NZ, NY, NC * LROWS, COLS), BF),
            pltpu.VMEM((CT, 512), BF),
            pltpu.VMEM((K, CT, COLS), F32),
            pltpu.VMEM(half, F32), pltpu.VMEM(half, F32),
            pltpu.VMEM(half, F32), pltpu.VMEM(half, F32),
            pltpu.VMEM(half, F32), pltpu.VMEM(half, F32),
            pltpu.VMEM((OWN, COLS), F32),
            pltpu.VMEM((OWN, COLS), BF),
            pltpu.VMEM((K, 128, 128), F32),
            pltpu.VMEM((K, 2, 8, 128), F32),
            pltpu.VMEM((K, 8, 8, 128), F32),
            pltpu.VMEM((K, 8, 8, 128), F32),
            pltpu.VMEM((128, 128), F32),
            pltpu.VMEM((128, 128), F32),
            pltpu.VMEM((256, 128), F32),
            pltpu.VMEM((TOK, COLS), BF),
            pltpu.VMEM((NZ, NC, LROWS, CT), F32),
            pltpu.VMEM((K, NY, NZ, LROWS, CT), F32),
            pltpu.VMEM((K, NY, NZ, LROWS, CT), BF),
            pltpu.VMEM((K, NY, NZ, LROWS, CT), BF),
            pltpu.VMEM((K, 6, NZ, LROWS, LH), BF),
            pltpu.VMEM((K, 6, NZ, LROWS, LH), BF),
            pltpu.VMEM((NZ, LROWS, CT), F32),
            pltpu.VMEM((K, NZ, LROWS, CT), BF),
            pltpu.VMEM((K, NZ, LROWS, CT), BF),
            pltpu.VMEM((K, LROWS, CT), F32),
            dma((6,)), dma((8,)),
            dma((NZ, 4)), dma((NZ, 4)),
            dma((K, 4)), dma((K, 4)),
            dma((K, NZ)), dma((K, NZ)),
            dma((K, 4)), dma((K, 4)),
            dma((K, 6)), dma((K, 6)),
            dma((K, 8)), dma((K, 8)),
            dma((K, 8)), dma((K, 8)),
            dma((K, 4)), dma((K, 4)),
            dma((K, 4)), dma((K, 4)),
            dma((K, 8)), dma((K, 8)),
            dma((K, 6)), dma((K, 6)),
        ],
        compiler_params=pltpu.CompilerParams(
            collective_id=0, has_side_effects=True, vmem_limit_bytes=56 * 1024 * 1024
        ),
    )(hidden_t, head.reshape(NZ, NY, NC * LROWS, COLS), teacher, labels.reshape(1, OWN), temps, mix)


def solution(mesh):
    placed = (P(("dp", "vocab"), None), P("dp", "vocab"), P("dp", "vocab"), P("dp"), P(), P())
    return jax.shard_map(
        shards,
        mesh=mesh,
        in_specs=placed,
        out_specs=(P(("dp", "vocab"), None), P("dp", "vocab")),
        check_vma=False,
    )
```

time: 138 us -> 106 us (0.77)
  Pallas kernels: 129 us -> 101 us
  local copies, waits for them, and re-layouts: 6.72 us -> 3 us
    pallas_call x1, Pallas kernels: 129 us -> 101 us  [shards(): pl.pallas_call(body, out_shape=(pltpu.VMEM((LROWS, TOK), F32), pltpu.VMEM...]
    unnamed x2, local copies, waits for them, and re-layouts: 6.72 us -> 3 us
where the time goes in v4:
time: 106 us; the launch traced here: 105 us
  Pallas kernels  101 us (95%)
  local copies, waits for them, and re-layouts  3 us (3%)
    pallas_call x1, Pallas kernels, shards(): pl.pallas_call(body, out_shape=(pltpu.VMEM((LROWS, TOK), F32), pltpu.VMEM...  101 us
    unnamed x2, local copies, waits for them, and re-layouts  3 us

profile of v4, /device:TPU:2, one launch (start us, length us, event | category | flops | bytes accessed | tf_op | source)
XLA Modules:
  0.0 104.7 jit_solution(13142831100543387094)
XLA Ops:
  0.6 101.1 %shard_map.77 = (f32[32,768]{1,0:T(8,128)S(1)}, bf16[2048,1280]{1,0:T(8,128)(2,1)S(1)}) custom-call(bf16[32,768]{1,0:T(8,128)(2,1)} %hid_hbm.1, bf16[8,4,64,1280]{3,2,1,0:T(8,128)(2,1)} %bitcast.2, bf16[192,1280]{1,0:T(8,128)(2,1)} %teach_hbm.1, s32[1,192]{1,0:T(1,128)} %bitcast.3, f32[4]{0:T(128)} %temps_hbm.1, f32[2]{0:T(128)} %mix_hbm.1), custom_call_target="tpu_custom_call" | custom-call | tf_op jit(solution)/shard_map/pallas_call | solution.py:505
  101.7 0.6 copy.10
  102.4 2.4 %copy.11 = bf16[2048,1280]{1,0:T(8,128)(2,1)} copy(bf16[2048,1280]{1,0:T(8,128)(2,1)S(1)} %get-tuple-element.3) | data formatting | bytes 10485760

commit v5 on v4

--- a/solution.py
+++ b/solution.py
@@ -24,10 +24,10 @@
 
 def body(hid_hbm, head_hbm, teach_hbm, labels_hbm, temps_hbm, mix_hbm,
          hgrad, hdgrad,
-         hid, labels, temps, mix, hdo,
-         hb, hd, ht, part, ra1, rb1, ra2, rb2, ra3, rb3, logit, teach,
+         hid, labels, temps, mix,
+         hb, hd, ht, part, ra1, rb1, rr, logit, teach,
          wt, st, r1, r2, ct, coef, lab, grads, tmp, hgo, ps, pr, ysb, yrb, ysum, zsb, zrb, res,
-         loc_sem, out_sem, fy_s, fy_r, ay_s, ay_r, az_s, az_r, ap_s, ap_r,
+         loc_sem, fy_s, fy_r, fq_r, ay_s, ay_r, az_s, az_r, ap_s, ap_r,
          rx_s, rx_r, s1_s, s1_r, s2_s, s2_r, gx_s, gx_r,
          pp_s, pp_r, zz_s, zz_r, yy_s, yy_r):
     x = lax.axis_index("dp")
@@ -60,15 +60,22 @@
     def group2(k):
         return vid(zrel(k), y, c)
 
-    sent = []
-
     def send(src, dst, ssem, rsem, dev):
         cp = pltpu.make_async_remote_copy(
             src_ref=src, dst_ref=dst, send_sem=ssem, recv_sem=rsem,
             device_id=dev, device_id_type=MESH)
         cp.start()
-        sent.append(cp)
         return cp
+
+    def all_in(ref, sem):
+        pltpu.make_async_remote_copy(
+            src_ref=ref, dst_ref=ref, send_sem=sem, recv_sem=sem,
+            device_id=mate, device_id_type=MESH).wait_recv()
+
+    def all_out(ref, sem):
+        pltpu.make_async_remote_copy(
+            src_ref=ref, dst_ref=ref, send_sem=sem, recv_sem=sem,
+            device_id=mate, device_id_type=MESH).wait_send()
 
     small = []
     for n, (a, b) in enumerate(((hid_hbm, hid), (labels_hbm, labels), (temps_hbm, temps), (mix_hbm, mix))):
@@ -107,20 +114,20 @@
     def zsend(k):
         own = hb.at[k, z, y, c]
         for i in range(1, NZ):
-            zin[k, i] = send(own, own, az_s.at[k, i], az_r.at[k, i], group2(i))
+            zin[k, i] = send(own, own, az_s.at[k], az_r.at[i - 1 if k == 0 else 6 + k], group2(i))
 
     def piece_out(i):
         b = hb.at[0, zrel(-i), y, c]
-        fin[i, 0] = send(b, b, fy_s.at[i, 0], fy_r.at[i, 0], yup)
-        fin[i, 1] = send(b, b, fy_s.at[i, 1], fy_r.at[i, 1], ydn)
+        fin[i, 0] = send(b, b, fy_s.at[0], fy_r.at[i, 0], yup)
+        fin[i, 1] = send(b, b, fy_s.at[1], fy_r.at[i, 1], ydn)
 
     def piece_on(i):
         fin[i, 0].wait_recv()
         b = hb.at[0, zrel(-i), yrel(-1), c, :, pl.ds(0, LH)]
-        fin[i, 2] = send(b, b, fy_s.at[i, 2], fy_r.at[i, 2], yup)
+        send(b, b, fy_s.at[2], fq_r.at[0], yup)
         fin[i, 1].wait_recv()
         b = hb.at[0, zrel(-i), yrel(1), c, :, pl.ds(LH, LH)]
-        fin[i, 3] = send(b, b, fy_s.at[i, 3], fy_r.at[i, 3], ydn)
+        send(b, b, fy_s.at[3], fq_r.at[1], ydn)
 
     zsend(0)
     piece_out(0)
@@ -167,29 +174,27 @@
 
     def give(k, i):
         b = bundle(k, GATHER[i])
-        gives[k, i] = send(b, b, ap_s.at[k, i], ap_r.at[k, i], mate)
+        gives[k, i] = send(b, b, ap_s.at[k], ap_r.at[k, i], mate)
 
     def yfirst(k):
-        for i in range(1, NZ):
-            zin[k, i].wait_recv()
+        all_in(hb.at[k, pl.ds(0, NZ - 1), y, c], az_r.at[6 + k])
         b = bundle(k, 0)
-        yin[k, 0] = send(b, b, ay_s.at[k, 0], ay_r.at[k, 0], yup)
-        yin[k, 1] = send(b, b, ay_s.at[k, 1], ay_r.at[k, 1], ydn)
+        yin[k, 0] = send(b, b, ay_s.at[k - 1], ay_r.at[k - 1, 0], yup)
+        yin[k, 1] = send(b, b, ay_s.at[k - 1], ay_r.at[k - 1, 1], ydn)
         give(k, 0)
 
     def ysecond(k):
         yin[k, 0].wait_recv()
         b = hb.at[k, :, yrel(-1), c, :, pl.ds(0, LH)]
-        yin[k, 2] = send(b, b, ay_s.at[k, 2], ay_r.at[k, 2], yup)
+        send(b, b, ay_s.at[k - 1], ay_r.at[k - 1, 2], yup)
         yin[k, 1].wait_recv()
         b = hb.at[k, :, yrel(1), c, :, pl.ds(LH, LH)]
-        yin[k, 3] = send(b, b, ay_s.at[k, 3], ay_r.at[k, 3], ydn)
+        send(b, b, ay_s.at[k - 1], ay_r.at[k - 1, 2], ydn)
         give(k, 1)
         give(k, 2)
 
     def ythird(k):
-        yin[k, 2].wait_recv()
-        yin[k, 3].wait_recv()
+        all_in(hb.at[k, :, yrel(2), c], ay_r.at[k - 1, 2])
         give(k, 3)
 
     def stage(k, i):
@@ -210,32 +215,29 @@
     flying = {}
 
     def far(k):
-        flying[k, 0] = send(part.at[k, tokens(2, 0)], ra1.at[k], rx_s.at[k, 0], rx_r.at[k, 0], xup)
-        flying[k, 1] = send(part.at[k, tokens(2, 1)], rb1.at[k], rx_s.at[k, 1], rx_r.at[k, 1], xdn)
+        flying[k, 0] = send(part.at[k, tokens(2, 0)], ra1.at[k], rx_s.at[k], rx_r.at[k, 0], xup)
+        flying[k, 1] = send(part.at[k, tokens(2, 1)], rb1.at[k], rx_s.at[k], rx_r.at[k, 1], xdn)
 
     def near(k):
-        flying[k, 2] = send(part.at[k, tokens(1, 1)], rb2.at[k], rx_s.at[k, 2], rx_r.at[k, 2], xup)
-        flying[k, 3] = send(part.at[k, tokens(-1, 0)], ra2.at[k], rx_s.at[k, 3], rx_r.at[k, 3], xdn)
+        send(part.at[k, tokens(1, 1)], rr.at[k, 0], rx_s.at[k], rx_r.at[k, 2], xup)
+        send(part.at[k, tokens(-1, 0)], rr.at[k, 1], rx_s.at[k], rx_r.at[k, 2], xdn)
 
     def relay(k):
         flying[k, 0].wait_recv()
         ra1[k] = ra1[k] + part[k, tokens(1, 0), :]
-        flying[k, 4] = send(ra1.at[k], ra3.at[k], rx_s.at[k, 4], rx_r.at[k, 4], xup)
+        send(ra1.at[k], rr.at[k, 2], rx_s.at[k], rx_r.at[k, 2], xup)
         flying[k, 1].wait_recv()
         rb1[k] = rb1[k] + part[k, tokens(-1, 1), :]
-        flying[k, 5] = send(rb1.at[k], rb3.at[k], rx_s.at[k, 5], rx_r.at[k, 5], xdn)
+        send(rb1.at[k], rr.at[k, 3], rx_s.at[k], rx_r.at[k, 2], xdn)
 
     def final(k):
-        for i in (2, 3, 4, 5):
-            flying[k, i].wait_recv()
-        logit[pl.ds(k * GT, GH), :] = part[k, tokens(0, 0), :] + ra2[k] + ra3[k]
-        logit[pl.ds(k * GT + GH, GH), :] = part[k, tokens(0, 1), :] + rb2[k] + rb3[k]
-
-    swaps = {}
+        all_in(rr.at[k], rx_r.at[k, 2])
+        logit[pl.ds(k * GT, GH), :] = part[k, tokens(0, 0), :] + rr[k, 1] + rr[k, 2]
+        logit[pl.ds(k * GT + GH, GH), :] = part[k, tokens(0, 1), :] + rr[k, 0] + rr[k, 3]
 
     def exchange(k, src, dst, ssem, rsem, group):
-        swaps[k] = [send(src, dst.at[k, i], ssem.at[k, i], rsem.at[k, i], group(i))
-                    for i in range(1, 8)]
+        for i in range(1, 8):
+            send(src, dst.at[k, i], ssem.at[k], rsem.at[k], group(i))
 
     def local_stats(k):
         @pl.loop(0, GT // 32)
@@ -254,9 +256,8 @@
         st[k, 0] = jnp.where(left, flat[0:8, :], pltpu.roll(flat[8:16, :], 64, 1))
         exchange(k, st.at[k, 0], r1, s1_s, s1_r, group1)
 
-    def merge(k, mine, got):
-        for f in swaps[k]:
-            f.wait_recv()
+    def merge(k, mine, got, rsem):
+        all_in(got.at[k, pl.ds(1, 7)], rsem.at[k])
         all_s = [st[k, mine]] + [got[k, i] for i in range(1, 8)]
         top = all_s[0][0:1, :]
         for s in all_s[1:]:
@@ -268,7 +269,7 @@
         return top, acc
 
     def merge1(k):
-        top, acc = merge(k, 0, r1)
+        top, acc = merge(k, 0, r1, s1_r)
         st[k, 1] = jnp.where(row2 == 0, top, acc)
         exchange(k, st.at[k, 1], r2, s2_s, s2_r, group2)
 
@@ -276,7 +277,7 @@
     col = lax.broadcasted_iota(jnp.int32, (32, CW), 1).astype(F32)
 
     def grad(k):
-        top, acc = merge(k, 1, r2)
+        top, acc = merge(k, 1, r2, s2_r)
         acc = jnp.where(wcol > 0.0, acc, 1.0)
         both = jnp.where(row2 == 0, top, wcol / acc)
         ct[pl.ds(0, 8), :] = both
@@ -303,20 +304,19 @@
                 grads[out, cc] = g.astype(BF)
 
         b = grads.at[pl.ds(pl.multiple_of(k * CT + x * GT, GT), GT)]
-        flying[k, 6] = send(b, b, gx_s.at[k, 0], gx_r.at[k, 0], xup)
-        flying[k, 7] = send(b, b, gx_s.at[k, 1], gx_r.at[k, 1], xdn)
+        flying[k, 6] = send(b, b, gx_s.at[k], gx_r.at[k, 0], xup)
+        flying[k, 7] = send(b, b, gx_s.at[k], gx_r.at[k, 1], xdn)
 
     def passon(k):
         a = grads.at[pl.ds(pl.multiple_of(k * CT + xrel(-1) * GT, GH), GH)]
         b = grads.at[pl.ds(pl.multiple_of(k * CT + xrel(1) * GT + GH, GH), GH)]
         flying[k, 6].wait_recv()
-        flying[k, 8] = send(a, a, gx_s.at[k, 2], gx_r.at[k, 2], xup)
+        send(a, a, gx_s.at[k], gx_r.at[k, 2], xup)
         flying[k, 7].wait_recv()
-        flying[k, 9] = send(b, b, gx_s.at[k, 3], gx_r.at[k, 3], xdn)
+        send(b, b, gx_s.at[k], gx_r.at[k, 2], xdn)
 
     def landed(k):
-        for i in (8, 9):
-            flying[k, i].wait_recv()
+        all_in(grads.at[pl.ds(pl.multiple_of(k * CT + xrel(2) * GT, GT), GT)], gx_r.at[k, 2])
 
     pairs = {}
 
@@ -327,7 +327,7 @@
         tmp[...] = r.reshape(NZ, NC, LROWS, CT)
         hgo[k, i] = tmp[:, c]
         ps[k, i] = tmp[:, 1 - c].astype(BF)
-        pairs[k, i] = send(ps.at[k, i], pr.at[k, i], pp_s.at[k, i], pp_r.at[k, i], mate)
+        pairs[k, i] = send(ps.at[k, i], pr.at[k, i], pp_s.at[k], pp_r.at[k, i], mate)
 
     LO, HI = pl.ds(0, LH), pl.ds(LH, LH)
 
@@ -338,7 +338,7 @@
 
     def yhop(k, i, val, dev):
         ysb[k, i] = val.astype(BF)
-        hops[k, i] = send(ysb.at[k, i], yrb.at[k, i], yy_s.at[k, i], yy_r.at[k, i], dev)
+        hops[k, i] = send(ysb.at[k, i], yrb.at[k, i], yy_s.at[k], yy_r.at[k, min(i, 2)], dev)
 
     def scatter(k, step):
         if step == 0:
@@ -357,24 +357,19 @@
             yhop(k, 5, total(k, 2, HI) + yrb[k, 1].astype(F32), ydn)
         elif step == 3:
             pairs[k, 3].wait_recv()
-            for i in (2, 3, 4, 5):
-                hops[k, i].wait_recv()
+            all_in(yrb.at[k, pl.ds(2, 4)], yy_r.at[k, 2])
             ysum[:, :, LO] = total(k, 3, LO) + yrb[k, 3].astype(F32) + yrb[k, 4].astype(F32)
             ysum[:, :, HI] = total(k, 3, HI) + yrb[k, 2].astype(F32) + yrb[k, 5].astype(F32)
             zsb[k] = ysum[...].astype(BF)
             res[k] = ysum[z]
             for i in range(1, NZ):
-                hops[k, "z", i] = send(zsb.at[k, zrel(i)], zrb.at[k, i],
-                                       zz_s.at[k, i], zz_r.at[k, i], group2(i))
+                send(zsb.at[k, zrel(i)], zrb.at[k, i], zz_s.at[k], zz_r.at[k], group2(i))
         else:
-            for i in range(1, NZ):
-                hops[k, "z", i].wait_recv()
+            all_in(zrb.at[k, pl.ds(1, NZ - 1)], zz_r.at[k])
             acc = res[k]
             for i in range(1, NZ):
                 acc = acc + zrb[k, i].astype(F32)
             res[k] = acc
-
-    outs = []
 
     def head_part(b):
         for j in range(NCH):
@@ -384,30 +379,28 @@
                 t = jnp.dot(hb[k, b].reshape(256, CT), grads[pl.ds(k * CT, CT), cc],
                             preferred_element_type=F32)
                 r = t if r is None else r + t
-            hdo[pl.ds(b * 256, 256), cc] = r.astype(BF)
-        rows = pl.ds(b * 256, 256)
-        outs.append(pltpu.make_async_copy(hdo.at[rows], hdgrad.at[rows], out_sem.at[b]))
-        outs[-1].start()
+            hdgrad[pl.ds(b * 256, 256), cc] = r.astype(BF)
 
     NEAREST = (1, 7, 2, 6, 3, 5, 4)
     for i in NEAREST:
         zin[0, i].wait_recv()
         piece_out(i)
+        if i == 7:
+            zsend(1)
     give(0, 0)
-    zsend(1)
+    zsend(2)
     for i in (0,) + NEAREST:
         piece_on(i)
     give(0, 1)
     give(0, 2)
-    zsend(2)
     head_copy.wait()
     stage(0, 0)
     yfirst(1)
     stage(0, 1)
     stage(0, 2)
-    for i in (0,) + NEAREST:
-        fin[i, 2].wait_recv()
-        fin[i, 3].wait_recv()
+    far_y = hb.at[0, :, yrel(2), c]
+    all_in(far_y.at[:, :, pl.ds(0, LH)], fq_r.at[0])
+    all_in(far_y.at[:, :, pl.ds(LH, LH)], fq_r.at[1])
     give(0, 3)
     stage(0, 3)
     far(0)
@@ -418,8 +411,8 @@
     yfirst(2)
     stage(1, 1)
     stage(1, 2)
+    relay(0)
     ythird(1)
-    relay(0)
     stage(1, 3)
     far(1)
     near(1)
@@ -444,8 +437,8 @@
     final(2)
     local_stats(2)
     passon(0)
+    grad(1)
     merge1(2)
-    grad(1)
     landed(0)
     pair(0, 0)
     pair(0, 1)
@@ -461,27 +454,28 @@
     pair(1, 1)
     scatter(1, 0)
     passon(2)
-    scatter(0, 3)
     pair(1, 2)
     pair(1, 3)
     scatter(1, 1)
     landed(2)
     pair(2, 0)
+    scatter(0, 3)
     scatter(1, 2)
     pair(2, 1)
     pair(2, 2)
     scatter(2, 0)
     pair(2, 3)
-    scatter(1, 3)
     scatter(2, 1)
     head_part(0)
     head_part(1)
+    head_part(2)
     scatter(2, 2)
-    head_part(2)
+    scatter(1, 3)
     head_part(3)
     head_part(4)
+    head_part(5)
     scatter(2, 3)
-    for b in (5, 6, 7):
+    for b in (6, 7):
         head_part(b)
     scatter(0, 4)
     scatter(1, 4)
@@ -491,10 +485,22 @@
     hgrad[...] = jnp.concatenate(
         [full[k][:, d * GT:(d + 1) * GT] for d in range(NX) for k in range(K)], axis=1)
 
-    for cp in sent:
-        cp.wait_send()
-    for cp in outs:
-        cp.wait()
+    one = hb.at[0, :, y, c]
+    for i in (0, 1):
+        all_out(one, fy_s.at[i])
+        all_out(one.at[:, :, pl.ds(0, LH)], fy_s.at[2 + i])
+    for k in range(K):
+        all_out(hb.at[k, pl.ds(0, NZ - 1), y, c], az_s.at[k])
+        all_out(hb.at[k, :, :, c], ap_s.at[k])
+        if k > 0:
+            all_out(hb.at[k, :, pl.ds(0, 3), c], ay_s.at[k - 1])
+        all_out(logit, rx_s.at[k])
+        all_out(r1.at[k, pl.ds(1, 7)], s1_s.at[k])
+        all_out(r2.at[k, pl.ds(1, 7)], s2_s.at[k])
+        all_out(grads.at[pl.ds(0, OWN)], gx_s.at[k])
+        all_out(ps.at[k], pp_s.at[k])
+        all_out(ysb.at[k], yy_s.at[k])
+        all_out(zrb.at[k, pl.ds(1, NZ - 1)], zz_s.at[k])
 
 
 def shards(hidden_t, head, teacher, labels, temps, mix):
@@ -509,20 +515,18 @@
             pltpu.VMEM((FEAT, COLS), BF),
         ),
         in_specs=[hbm] * 6,
-        out_specs=(vmem, hbm),
+        out_specs=(vmem, vmem),
         scratch_shapes=[
             pltpu.VMEM((LROWS, TOK), BF),
             pltpu.VMEM((1, OWN), jnp.int32),
             pltpu.SMEM((NT,), F32),
             pltpu.SMEM((2,), F32),
-            pltpu.VMEM((FEAT, COLS), BF),
             pltpu.VMEM((K, NZ, NY, NC, LROWS, CT), BF),
             pltpu.VMEM((NZ, NY, NC * LROWS, COLS), BF),
             pltpu.VMEM((CT, 512), BF),
             pltpu.VMEM((K, CT, COLS), F32),
             pltpu.VMEM(half, F32), pltpu.VMEM(half, F32),
-            pltpu.VMEM(half, F32), pltpu.VMEM(half, F32),
-            pltpu.VMEM(half, F32), pltpu.VMEM(half, F32),
+            pltpu.VMEM((K, 4, GH, COLS), F32),
             pltpu.VMEM((OWN, COLS), F32),
             pltpu.VMEM((OWN, COLS), BF),
             pltpu.VMEM((K, 128, 128), F32),
@@ -543,18 +547,18 @@
             pltpu.VMEM((K, NZ, LROWS, CT), BF),
             pltpu.VMEM((K, NZ, LROWS, CT), BF),
             pltpu.VMEM((K, LROWS, CT), F32),
-            dma((6,)), dma((8,)),
-            dma((NZ, 4)), dma((NZ, 4)),
-            dma((K, 4)), dma((K, 4)),
-            dma((K, NZ)), dma((K, NZ)),
-            dma((K, 4)), dma((K, 4)),
-            dma((K, 6)), dma((K, 6)),
-            dma((K, 8)), dma((K, 8)),
-            dma((K, 8)), dma((K, 8)),
-            dma((K, 4)), dma((K, 4)),
-            dma((K, 4)), dma((K, 4)),
-            dma((K, 8)), dma((K, 8)),
-            dma((K, 6)), dma((K, 6)),
+            dma((6,)),
+            dma((4,)), dma((NZ, 2)), dma((2,)),
+            dma((K - 1,)), dma((K - 1, 3)),
+            dma((K,)), dma((6 + K,)),
+            dma((K,)), dma((K, 4)),
+            dma((K,)), dma((K, 3)),
+            dma((K,)), dma((K,)),
+            dma((K,)), dma((K,)),
+            dma((K,)), dma((K, 3)),
+            dma((K,)), dma((K, 4)),
+            dma((K,)), dma((K,)),
+            dma((K,)), dma((K, 3)),
         ],
         compiler_params=pltpu.CompilerParams(
             collective_id=0, has_side_effects=True, vmem_limit_bytes=56 * 1024 * 1024

time: 106 us -> 101 us (0.953)
  Pallas kernels: 101 us -> 97.1 us
    pallas_call x1, Pallas kernels: 101 us -> 97.1 us  [shards(): pl.pallas_call(body, out_shape=(pltpu.VMEM((LROWS, TOK), F32), pltpu.VMEM...]
where the time goes in v5:
time: 101 us
  Pallas kernels  97.1 us (96%)
  local copies, waits for them, and re-layouts  3 us (3%)
    pallas_call x1, Pallas kernels, shards(): pl.pallas_call(body, out_shape=(pltpu.VMEM((LROWS, TOK), F32), pltpu.VMEM...  97.1 us
    unnamed x2, local copies, waits for them, and re-layouts  3 us

profile of v5, /device:TPU:2, one launch (start us, length us, event | category | flops | bytes accessed | tf_op | source)
XLA Modules:
  0.0 100.8 jit_solution(14425292553648504150)
XLA Ops:
  0.6 97.1 %shard_map.77 = (f32[32,768]{1,0:T(8,128)S(1)}, bf16[2048,1280]{1,0:T(8,128)(2,1)S(1)}) custom-call(bf16[32,768]{1,0:T(8,128)(2,1)} %hid_hbm.1, bf16[8,4,64,1280]{3,2,1,0:T(8,128)(2,1)} %bitcast.2, bf16[192,1280]{1,0:T(8,128)(2,1)} %teach_hbm.1, s32[1,192]{1,0:T(1,128)} %bitcast.3, f32[4]{0:T(128)} %temps_hbm.1, f32[2]{0:T(128)} %mix_hbm.1), custom_call_target="tpu_custom_call" | custom-call | tf_op jit(solution)/shard_map/pallas_call | solution.py:511
  97.8 0.6 copy.10
  98.4 2.4 %copy.11 = bf16[2048,1280]{1,0:T(8,128)(2,1)} copy(bf16[2048,1280]{1,0:T(8,128)(2,1)S(1)} %get-tuple-element.3) | data formatting | bytes 10485760

commit v6 on v5

--- a/solution.py
+++ b/solution.py
@@ -20,6 +20,8 @@
 NT = 4
 GATHER = (0, -1, 1, 2)
 SPREAD = (2, 1, -1, 0)
+FARTHEST = (4, 3, 5, 2, 6, 1, 7)
+PARTS = (((0, 5),), ((0, 5),), ((0, 3), (3, 5)))
 
 
 def body(hid_hbm, head_hbm, teach_hbm, labels_hbm, temps_hbm, mix_hbm,
@@ -113,7 +115,7 @@
 
     def zsend(k):
         own = hb.at[k, z, y, c]
-        for i in range(1, NZ):
+        for i in FARTHEST:
             zin[k, i] = send(own, own, az_s.at[k], az_r.at[i - 1 if k == 0 else 6 + k], group2(i))
 
     def piece_out(i):
@@ -236,7 +238,7 @@
         logit[pl.ds(k * GT + GH, GH), :] = part[k, tokens(0, 1), :] + rr[k, 0] + rr[k, 3]
 
     def exchange(k, src, dst, ssem, rsem, group):
-        for i in range(1, 8):
+        for i in FARTHEST:
             send(src, dst.at[k, i], ssem.at[k], rsem.at[k], group(i))
 
     def local_stats(k):
@@ -285,49 +287,68 @@
         ct[pl.ds(16, 112), :] = jnp.zeros((112, 128), F32)
         coef[...] = ct[...].T
 
-        for i in range(GT // 32):
-            cf = coef[pl.ds(i * 32, 32), :]
-            r = pl.ds(k * GT + i * 32, 32)
-            lb = lab[r, 0:1]
-
-            @pl.loop(0, NCH)
-            def _(j):
-                cc = pl.ds(pl.multiple_of(j * CW, CW), CW)
-                s = logit[r, cc] - cf[:, 0:1]
-                t = teach[r, cc].astype(F32) - cf[:, 8:9]
-                g = cf[:, 1:2] * jnp.exp(s)
-                g = g - jnp.where(col + (base + j * CW).astype(F32) == lb, mix[0], 0.0)
-                for q in range(NT):
-                    g = g + cf[:, 2 + q:3 + q] * jnp.exp(s * inv[q])
-                    g = g - cf[:, 9 + q:10 + q] * jnp.exp(t * inv[q])
-                out = pl.ds(pl.multiple_of(k * CT + x * GT + i * 32, 32), 32)
-                grads[out, cc] = g.astype(BF)
-
-        b = grads.at[pl.ds(pl.multiple_of(k * CT + x * GT, GT), GT)]
-        flying[k, 6] = send(b, b, gx_s.at[k], gx_r.at[k, 0], xup)
-        flying[k, 7] = send(b, b, gx_s.at[k], gx_r.at[k, 1], xdn)
-
-    def passon(k):
-        a = grads.at[pl.ds(pl.multiple_of(k * CT + xrel(-1) * GT, GH), GH)]
-        b = grads.at[pl.ds(pl.multiple_of(k * CT + xrel(1) * GT + GH, GH), GH)]
-        flying[k, 6].wait_recv()
-        send(a, a, gx_s.at[k], gx_r.at[k, 2], xup)
-        flying[k, 7].wait_recv()
-        send(b, b, gx_s.at[k], gx_r.at[k, 2], xdn)
+        for p, (j0, j1) in enumerate(PARTS[k]):
+            for i in range(GT // 32):
+                cf = coef[pl.ds(i * 32, 32), :]
+                r = pl.ds(k * GT + i * 32, 32)
+                lb = lab[r, 0:1]
+
+                @pl.loop(j0, j1)
+                def _(j):
+                    cc = pl.ds(pl.multiple_of(j * CW, CW), CW)
+                    s = logit[r, cc] - cf[:, 0:1]
+                    t = teach[r, cc].astype(F32) - cf[:, 8:9]
+                    g = cf[:, 1:2] * jnp.exp(s)
+                    g = g - jnp.where(col + (base + j * CW).astype(F32) == lb, mix[0], 0.0)
+                    for q in range(NT):
+                        g = g + cf[:, 2 + q:3 + q] * jnp.exp(s * inv[q])
+                        g = g - cf[:, 9 + q:10 + q] * jnp.exp(t * inv[q])
+                    out = pl.ds(pl.multiple_of(k * CT + x * GT + i * 32, 32), 32)
+                    grads[out, cc] = g.astype(BF)
+
+            b = gview(k, p, x * GT, GT)
+            flying[k, "g", p, 0] = send(b, b, gx_s.at[k], gx_r.at[k, 3 * p], xup)
+            flying[k, "g", p, 1] = send(b, b, gx_s.at[k], gx_r.at[k, 3 * p + 1], xdn)
+
+    def gview(k, p, row, rows):
+        j0, j1 = PARTS[k][p]
+        return grads.at[pl.ds(pl.multiple_of(k * CT + row, GH), rows), pl.ds(j0 * CW, (j1 - j0) * CW)]
+
+    def passon(k, p=0):
+        flying[k, "g", p, 0].wait_recv()
+        a = gview(k, p, xrel(-1) * GT, GH)
+        send(a, a, gx_s.at[k], gx_r.at[k, 3 * p + 2], xup)
+        flying[k, "g", p, 1].wait_recv()
+        b = gview(k, p, xrel(1) * GT + GH, GH)
+        send(b, b, gx_s.at[k], gx_r.at[k, 3 * p + 2], xdn)
 
     def landed(k):
-        all_in(grads.at[pl.ds(pl.multiple_of(k * CT + xrel(2) * GT, GT), GT)], gx_r.at[k, 2])
+        for p in range(len(PARTS[k])):
+            all_in(gview(k, p, xrel(2) * GT, GT), gx_r.at[k, 3 * p + 2])
 
     pairs = {}
 
     def pair(k, i):
         yb = yrel(SPREAD[i])
-        r = lax.dot_general(hd[:, yb].reshape(512, COLS), grads[pl.ds(k * CT, CT), :],
-                            (((1,), (1,)), ((), ())), preferred_element_type=F32)
-        tmp[...] = r.reshape(NZ, NC, LROWS, CT)
-        hgo[k, i] = tmp[:, c]
-        ps[k, i] = tmp[:, 1 - c].astype(BF)
+
+        def rows_of(cc):
+            w = hd[:, yb, pl.ds(pl.multiple_of(cc * LROWS, LROWS), LROWS), :]
+            r = lax.dot_general(w.reshape(256, COLS), grads[pl.ds(k * CT, CT), :],
+                                (((1,), (1,)), ((), ())), preferred_element_type=F32)
+            return r.reshape(NZ, LROWS, CT)
+
+        if (k, i) == (K - 1, 0):
+            ps[k, i] = rows_of(1 - c).astype(BF)
+        else:
+            r = lax.dot_general(hd[:, yb].reshape(512, COLS), grads[pl.ds(k * CT, CT), :],
+                                (((1,), (1,)), ((), ())), preferred_element_type=F32)
+            tmp[...] = r.reshape(NZ, NC, LROWS, CT)
+            ps[k, i] = tmp[:, 1 - c].astype(BF)
         pairs[k, i] = send(ps.at[k, i], pr.at[k, i], pp_s.at[k], pp_r.at[k, i], mate)
+        if (k, i) == (K - 1, 0):
+            hgo[k, i] = rows_of(c)
+        else:
+            hgo[k, i] = tmp[:, c]
 
     LO, HI = pl.ds(0, LH), pl.ds(LH, LH)
 
@@ -362,7 +383,7 @@
             ysum[:, :, HI] = total(k, 3, HI) + yrb[k, 2].astype(F32) + yrb[k, 5].astype(F32)
             zsb[k] = ysum[...].astype(BF)
             res[k] = ysum[z]
-            for i in range(1, NZ):
+            for i in FARTHEST:
                 send(zsb.at[k, zrel(i)], zrb.at[k, i], zz_s.at[k], zz_r.at[k], group2(i))
         else:
             all_in(zrb.at[k, pl.ds(1, NZ - 1)], zz_r.at[k])
@@ -453,17 +474,18 @@
     pair(1, 0)
     pair(1, 1)
     scatter(1, 0)
-    passon(2)
+    passon(2, 0)
     pair(1, 2)
+    passon(2, 1)
     pair(1, 3)
     scatter(1, 1)
     landed(2)
     pair(2, 0)
-    scatter(0, 3)
     scatter(1, 2)
     pair(2, 1)
+    scatter(2, 0)
+    scatter(0, 3)
     pair(2, 2)
-    scatter(2, 0)
     pair(2, 3)
     scatter(2, 1)
     head_part(0)
@@ -555,7 +577,7 @@
             dma((K,)), dma((K, 3)),
             dma((K,)), dma((K,)),
             dma((K,)), dma((K,)),
-            dma((K,)), dma((K, 3)),
+            dma((K,)), dma((K, 6)),
             dma((K,)), dma((K, 4)),
             dma((K,)), dma((K,)),
             dma((K,)), dma((K, 3)),

time: 101 us -> 101 us (level); the launches traced: 101 us -> 99.4 us
  Pallas kernels: 97.1 us -> 95.8 us
    pallas_call x1, Pallas kernels: 97.1 us -> 95.8 us  [shards(): pl.pallas_call(body, out_shape=(pltpu.VMEM((LROWS, TOK), F32), pltpu.VMEM...]
where the time goes in v6:
time: 101 us; the launch traced here: 99.4 us
  Pallas kernels  95.8 us (95%)
  local copies, waits for them, and re-layouts  3 us (3%)
    pallas_call x1, Pallas kernels, shards(): pl.pallas_call(body, out_shape=(pltpu.VMEM((LROWS, TOK), F32), pltpu.VMEM...  95.8 us
    unnamed x2, local copies, waits for them, and re-layouts  3 us

profile of v6, /device:TPU:2, one launch (start us, length us, event | category | flops | bytes accessed | tf_op | source)
XLA Modules:
  0.0 99.4 jit_solution(18152100672663049323)
XLA Ops:
  0.6 95.8 %shard_map.77 = (f32[32,768]{1,0:T(8,128)S(1)}, bf16[2048,1280]{1,0:T(8,128)(2,1)S(1)}) custom-call(bf16[32,768]{1,0:T(8,128)(2,1)} %hid_hbm.1, bf16[8,4,64,1280]{3,2,1,0:T(8,128)(2,1)} %bitcast.2, bf16[192,1280]{1,0:T(8,128)(2,1)} %teach_hbm.1, s32[1,192]{1,0:T(1,128)} %bitcast.3, f32[4]{0:T(128)} %temps_hbm.1, f32[2]{0:T(128)} %mix_hbm.1), custom_call_target="tpu_custom_call" | custom-call | tf_op jit(solution)/shard_map/pallas_call | solution.py:533
  96.4 0.6 copy.10
  97.1 2.4 %copy.11 = bf16[2048,1280]{1,0:T(8,128)(2,1)} copy(bf16[2048,1280]{1,0:T(8,128)(2,1)S(1)} %get-tuple-element.3) | data formatting | bytes 10485760

commit v7 on v6

--- a/solution.py
+++ b/solution.py
@@ -21,7 +21,7 @@
 GATHER = (0, -1, 1, 2)
 SPREAD = (2, 1, -1, 0)
 FARTHEST = (4, 3, 5, 2, 6, 1, 7)
-PARTS = (((0, 5),), ((0, 5),), ((0, 3), (3, 5)))
+PARTS = (((0, 5),), ((0, 3), (3, 5)), ((0, 3), (3, 5)))
 
 
 def body(hid_hbm, head_hbm, teach_hbm, labels_hbm, temps_hbm, mix_hbm,
@@ -464,8 +464,9 @@
     pair(0, 0)
     pair(0, 1)
     scatter(0, 0)
-    passon(1)
+    passon(1, 0)
     grad(2)
+    passon(1, 1)
     pair(0, 2)
     pair(0, 3)
     scatter(0, 1)

time: 101 us -> 103 us (1.020)
  Pallas kernels: 95.8 us -> 98 us
    pallas_call x1, Pallas kernels: 95.8 us -> 98 us  [shards(): pl.pallas_call(body, out_shape=(pltpu.VMEM((LROWS, TOK), F32), pltpu.VMEM...]
where the time goes in v7:
time: 103 us; the launch traced here: 102 us
  Pallas kernels  98 us (95%)
  local copies, waits for them, and re-layouts  3 us (3%)
    pallas_call x1, Pallas kernels, shards(): pl.pallas_call(body, out_shape=(pltpu.VMEM((LROWS, TOK), F32), pltpu.VMEM...  98 us
    unnamed x2, local copies, waits for them, and re-layouts  3 us

profile of v7, /device:TPU:2, one launch (start us, length us, event | category | flops | bytes accessed | tf_op | source)
XLA Modules:
  0.0 101.6 jit_solution(14526344781496058124)
XLA Ops:
  0.6 98.0 %shard_map.77 = (f32[32,768]{1,0:T(8,128)S(1)}, bf16[2048,1280]{1,0:T(8,128)(2,1)S(1)}) custom-call(bf16[32,768]{1,0:T(8,128)(2,1)} %hid_hbm.1, bf16[8,4,64,1280]{3,2,1,0:T(8,128)(2,1)} %bitcast.2, bf16[192,1280]{1,0:T(8,128)(2,1)} %teach_hbm.1, s32[1,192]{1,0:T(1,128)} %bitcast.3, f32[4]{0:T(128)} %temps_hbm.1, f32[2]{0:T(128)} %mix_hbm.1), custom_call_target="tpu_custom_call" | custom-call | tf_op jit(solution)/shard_map/pallas_call | solution.py:534
  98.6 0.6 copy.10
  99.3 2.4 %copy.11 = bf16[2048,1280]{1,0:T(8,128)(2,1)} copy(bf16[2048,1280]{1,0:T(8,128)(2,1)S(1)} %get-tuple-element.3) | data formatting | bytes 10485760
